TPU v7x, 256 devices: a whole 4x4x8 slice. The times are simulated.
256 devices in a mesh: comp: 4 (over y), gx: 8 (over x, z_lo), gy: 8 (over z_hi, core).
Axes of the slice: x: 4, y: 4, z: 8 (z_hi: 4, z_lo: 2; z = z_hi * 2 + z_lo), core: 2. Of those that a mesh axis runs over, the one named last changes fastest.
Arguments:
- zonal_flow_speed: float32 [64, 128, 1024], P('comp', 'gx', 'gy'), may hold values from -5 to 5
- meridional_flow_speed: float32 [64, 128, 1024], P('comp', 'gx', 'gy'), may hold values from -5 to 5
- thermal_anomaly: float32 [64, 128, 1024], P('comp', 'gx', 'gy'), may hold values from -6 to 6
- brine_anomaly_values: float32 [64, 128, 1024], P('comp', 'gx', 'gy'), may hold values from -6 to 6
- marine_indicator: int32 [128, 1024], P('gx', 'gy'), may hold values 0 or 1
- seafloor_layer: int32 [128, 1024], P('gx', 'gy'), may hold values from 1 to 64
- dissolved_species: float32 [24, 64, 8, 4, 4, 1024], P(None, None, 'gx', 'comp', None, 'gy'), may hold values from 0.05 to 2
- topmost_sunshine: float32 [8, 4, 4, 1024], P('gx', 'comp', None, 'gy'), may hold values from 0.3 to 3
- attenuation_coefficient: float32 [24], replicated, may hold values from 0.01 to 0.1
- peak_intake_speed: float32 [24], replicated, may hold values from 0.2 to 2
- feedstock_midpoint_constant: float32 [24], replicated, may hold values from 0.05 to 1
- photon_midpoint_constant: float32 [24], replicated, may hold values from 0.05 to 1
- stoichiometry_matrix: float32 [24, 24], replicated, may hold values from -1.25 to 1.25
Outputs:
- east_new: float32 [64, 128, 1024], P('comp', 'gx', 'gy')
- north_new: float32 [64, 128, 1024], P('comp', 'gx', 'gy')
- warmed_result: float32 [64, 128, 1024], P('comp', 'gx', 'gy')
- salt_mixed: float32 [64, 128, 1024], P('comp', 'gx', 'gy')
- buoyancy: float32 [64, 128, 1024], P('comp', 'gx', 'gy')
- result: float32 [24, 64, 8, 4, 4, 1024], P(None, None, 'gx', 'comp', None, 'gy')
All inputs are finite; a program needn't handle non-finite values. No bound on the sum of `marine_indicator` on one device may be relied on, other than what follows from the above.
Results may differ from a plain program's by a relative error of at most 0.00007.
Values sent between devices are 32-bit elements; how exact they have to be, the bound alone decides.
A program may use at most 128 MiB of HBM per device.

v0:
```python
import jax
import jax.numpy as jnp
from jax import lax
from jax.sharding import PartitionSpec as P

NSUB = 2


DT_FLOW = 0.1
CORIOLIS = 0.3
MIXING = 0.15
COURANT = 0.24
DT_BIO = 0.5
WARMING_FACTOR = 0.5
CLEAR_WATER = 0.5
HIGHEST = lax.Precision.HIGHEST


def padded(x, sides, width):
    edges = {}
    for axis, dim in sides:
        count, length = (lax.axis_size(axis), x.shape[dim])
        up = [(i, (i + 1) % count) for i in range(count - 1)]
        last = lax.slice_in_dim(x, length - width, length, axis=dim)
        first = lax.slice_in_dim(x, 0, width, axis=dim)
        edges[dim] = (
            lax.ppermute(last, axis, up),
            lax.ppermute(first, axis, [(b, a) for a, b in up]),
        )
    done = []
    for _, dim in sides:
        low, high = edges[dim]
        around = [(width, width) if d in done else (0, 0) for d in range(x.ndim)]
        x = jnp.concatenate([jnp.pad(low, around), x, jnp.pad(high, around)], axis=dim)
        done.append(dim)
    return x


def from_everyone(x, axis):
    copies = jnp.broadcast_to(x, (lax.axis_size(axis), *x.shape))
    return lax.all_to_all(copies, axis, split_axis=0, concat_axis=0, tiled=True)


def in_order(pieces, dim):
    dims = list(pieces.shape[1:])
    dims[dim] *= pieces.shape[0]
    return jnp.moveaxis(pieces, 0, dim).reshape(dims)


def collect(x, axis, dim):
    pieces = from_everyone(x, axis)
    return in_order(pieces, dim)


def from_behind(x, axis, by):
    count = lax.axis_size(axis)
    pairs = [(i, i + by) for i in range(count) if 0 <= i + by < count]
    return lax.ppermute(x, axis, pairs)


def passed_along(x, axis, by):
    count = lax.axis_size(axis)
    return lax.ppermute(x, axis, [(i, (i + by) % count) for i in range(count)])


def extended_2(cells, sides, width):
    for axis, dim in sides:
        count = lax.axis_size(axis)
        ends = count - 1
        head = lax.slice_in_dim(cells, 0, width, axis=dim)
        tail = lax.slice_in_dim(cells, cells.shape[dim] - width, cells.shape[dim], axis=dim)
        cells = jnp.concatenate(
            [
                lax.ppermute(tail, axis, [(i, (i + 1) % count) for i in range(ends)]),
                cells,
                lax.ppermute(head, axis, [((i + 1) % count, i) for i in range(ends)]),
            ],
            axis=dim,
        )
    return cells


def on_device(
    zonal_flow_speed,
    meridional_flow_speed,
    thermal_anomaly,
    brine_anomaly_values,
    marine_indicator,
    seafloor_layer,
    dissolved_species,
    topmost_sunshine,
    attenuation_coefficient,
    peak_intake_speed,
    feedstock_midpoint_constant,
    photon_midpoint_constant,
    stoichiometry_matrix,
):
    group_index = lax.axis_index("comp")
    group_count = lax.axis_size("comp")
    levels_dev, tile_rows, tile_cols = zonal_flow_speed.shape
    tracer_count = dissolved_species.shape[0]
    level_count = dissolved_species.shape[1]
    sub_rows = dissolved_species.shape[4]
    rimmed = padded(jnp.stack([marine_indicator, seafloor_layer]), (("gx", 1), ("gy", 2)), 1)
    depth_index = group_index * levels_dev + jnp.arange(levels_dev, dtype=jnp.int32)[:, None, None]
    wet_rimmed = ((rimmed[0][None] == 1) & (depth_index < rimmed[1][None])).astype(jnp.float32)
    submerged_indicator = wet_rimmed[:, 1:-1, 1:-1]
    face_east = wet_rimmed[:, :-1, 1:-1] * wet_rimmed[:, 1:, 1:-1]
    face_north = wet_rimmed[:, 1:-1, :-1] * wet_rimmed[:, 1:-1, 1:]
    open_east = face_east[:, 1:]
    open_north = face_north[:, :, 1:]
    seawater_heaviness = submerged_indicator * (-0.2 * thermal_anomaly + 0.8 * brine_anomaly_values)
    column_total = jnp.sum(seawater_heaviness, axis=0)
    totals = collect(column_total[None], "comp", 0)
    earlier_groups = (jnp.arange(group_count, dtype=jnp.int32) < group_index).astype(jnp.float32)
    offset = jnp.sum(totals * earlier_groups[:, None, None], axis=0)
    strict_lower = (jnp.arange(levels_dev)[:, None] > jnp.arange(levels_dev)[None, :]).astype(
        jnp.float32
    )
    depth_above = offset[None] + jnp.dot(
        strict_lower, seawater_heaviness.reshape(levels_dev, -1), precision=HIGHEST
    ).reshape(seawater_heaviness.shape)
    weight_of_overlying = depth_above + 0.5 * seawater_heaviness
    padded_field = padded(
        jnp.stack([thermal_anomaly, brine_anomaly_values, weight_of_overlying]),
        (("gx", 2), ("gy", 3)),
        1,
    )
    pressure_east = padded_field[2, :, 2:, 1:-1]
    pressure_north = padded_field[2, :, 1:-1, 2:]
    east_new = open_east * (
        zonal_flow_speed
        + DT_FLOW * (CORIOLIS * meridional_flow_speed - (pressure_east - weight_of_overlying))
    )
    north_new = open_north * (
        meridional_flow_speed
        + DT_FLOW * (-CORIOLIS * zonal_flow_speed - (pressure_north - weight_of_overlying))
    )
    east_column, north_column = (
        lax.all_to_all(east_new, "comp", split_axis=1, concat_axis=0, tiled=True),
        lax.all_to_all(north_new, "comp", split_axis=1, concat_axis=0, tiled=True),
    )
    scalar_pair = padded_field[:2]
    flux_east = face_east[None] * (scalar_pair[:, :, 1:, 1:-1] - scalar_pair[:, :, :-1, 1:-1])
    flux_north = face_north[None] * (scalar_pair[:, :, 1:-1, 1:] - scalar_pair[:, :, 1:-1, :-1])
    blended_couple = scalar_pair[:, :, 1:-1, 1:-1] + MIXING * (
        flux_east[:, :, 1:]
        - flux_east[:, :, :-1]
        + (flux_north[:, :, :, 1:] - flux_north[:, :, :, :-1])
    )
    thermal_blended = blended_couple[0]
    salt_mixed = blended_couple[1]
    courant_east = COURANT * jnp.tanh(east_column)
    courant_north = COURANT * jnp.tanh(north_column)
    row_start = group_index * sub_rows
    sea_rows = lax.dynamic_slice_in_dim(marine_indicator, row_start, sub_rows, 0)
    bottom_rows = lax.dynamic_slice_in_dim(seafloor_layer, row_start, sub_rows, 0)
    column_depth = jnp.arange(level_count, dtype=jnp.int32)[:, None, None]
    wet_column = ((sea_rows[None] == 1) & (column_depth < bottom_rows[None])).astype(jnp.float32)
    north_before = from_behind(courant_north[:, :, -1], "gy", 1)
    courant_faces = jnp.concatenate([north_before[:, :, None], courant_north], axis=2)

    def neighbour_row(edge_row, shift_by, edge_group):
        within = passed_along(edge_row, "comp", shift_by)
        across = from_behind(within, "gx", shift_by)
        return jnp.where(group_index == edge_group, across, within)

    tracer_field = dissolved_species.reshape(tracer_count, level_count, sub_rows, tile_cols)
    east_below = neighbour_row(courant_east[:, -1], 1, 0)
    east_faces = jnp.concatenate([east_below[:, None], courant_east], axis=1)
    for substep in range(NSUB):
        row_below = neighbour_row(tracer_field[:, :, -1], 1, 0)
        beyond = neighbour_row(tracer_field[:, :, 0], -1, group_count - 1)
        extended = jnp.concatenate(
            [row_below[:, :, None], tracer_field, beyond[:, :, None]], axis=2
        )
        flux_faces = (
            jnp.maximum(east_faces, 0.0) * extended[:, :, :-1]
            + jnp.minimum(east_faces, 0.0) * extended[:, :, 1:]
        )
        change_east = flux_faces[:, :, 1:] - flux_faces[:, :, :-1]
        north_field = extended_2(tracer_field, (("gy", 3),), 1)
        flux_column = (
            jnp.maximum(courant_faces, 0.0) * north_field[:, :, :, :-1]
            + jnp.minimum(courant_faces, 0.0) * north_field[:, :, :, 1:]
        )
        change_north = flux_column[:, :, :, 1:] - flux_column[:, :, :, :-1]
        tracer_field = wet_column * (tracer_field - change_east - change_north)
    layer_depth = 2.0 / level_count
    optical_step = layer_depth * (
        CLEAR_WATER
        + jnp.tensordot(attenuation_coefficient, tracer_field, axes=1, precision=HIGHEST)
    )
    strict_column = (jnp.arange(level_count)[:, None] > jnp.arange(level_count)[None, :]).astype(
        jnp.float32
    )
    optical_above = jnp.dot(
        strict_column, optical_step.reshape(level_count, -1), precision=HIGHEST
    ).reshape(optical_step.shape)
    transmitted = jnp.exp(-optical_above)
    surface = topmost_sunshine.reshape(sub_rows, tile_cols)[None]
    light_level = surface * transmitted * jnp.exp(-0.5 * optical_step)
    warming_step = wet_column * surface * transmitted * (1.0 - jnp.exp(-optical_step)) / layer_depth
    warming_reverse = lax.all_to_all(warming_step, "comp", split_axis=0, concat_axis=1, tiled=True)
    nutrient = tracer_field[0]
    uptake_rates = (
        peak_intake_speed[:, None, None, None]
        * (nutrient / (feedstock_midpoint_constant[:, None, None, None] + nutrient))
        * (light_level / (light_level + photon_midpoint_constant[:, None, None, None]))
        * tracer_field
    )
    change = jnp.tensordot(stoichiometry_matrix, uptake_rates, axes=1, precision=HIGHEST)
    result = tracer_field + DT_BIO * wet_column * change
    warmed_result = thermal_blended + WARMING_FACTOR * warming_reverse
    buoyancy = submerged_indicator * (0.2 * warmed_result - 0.8 * salt_mixed)
    return (
        east_new,
        north_new,
        warmed_result,
        salt_mixed,
        buoyancy,
        result.reshape(dissolved_species.shape),
    )


def solution(mesh):
    return jax.shard_map(
        on_device,
        mesh=mesh,
        in_specs=(
            P("comp", "gx", "gy"),
            P("comp", "gx", "gy"),
            P("comp", "gx", "gy"),
            P("comp", "gx", "gy"),
            P("gx", "gy"),
            P("gx", "gy"),
            P(None, None, "gx", "comp", None, "gy"),
            P("gx", "comp", None, "gy"),
            P(),
            P(),
            P(),
            P(),
            P(),
        ),
        out_specs=(
            P("comp", "gx", "gy"),
            P("comp", "gx", "gy"),
            P("comp", "gx", "gy"),
            P("comp", "gx", "gy"),
            P("comp", "gx", "gy"),
            P(None, None, "gx", "comp", None, "gy"),
        ),
        check_vma=False,
    )
```

profile of v0, /device:TPU:15, one launch (start us, length us, event | category | flops | bytes accessed | tf_op | source)
XLA Modules:
  0.0 252.4 jit_solution(14438228290551515185)
XLA Ops:
  1.5 2.6 %collective-permute-start.3 = (s32[2,16,1]{2,1,0:T(8,128)S(1)}, s32[2,16,1]{2,1,0:T(8,128)S(1)}, u32[]{:S(2)}, u32[]{:S(2)}) collective-permute-start(s32[2,16,1]{2,1,0:T(8,128)S(1)} %get-tuple-element.73), channel_id=1, source_target_pairs={{1,0},{2,1},{3,2},{4,3},{5,4},{6,5},{7,6},{9,8},{10,9},{11,10},{12... | collective-permute-start | bytes 392 | tf_op jit(solution)/shard_map/ppermute | solution.py:28
  4.1 4.8 %collective-permute-start = (s32[2,16,1]{2,1,0:T(8,128)S(1)}, s32[2,16,1]{2,1,0:T(8,128)S(1)}, u32[]{:S(2)}, u32[]{:S(2)}) collective-permute-start(s32[2,16,1]{2,1,0:T(8,128)S(1)} %get-tuple-element.72), channel_id=1, source_target_pairs={{0,1},{1,2},{2,3},{3,4},{4,5},{5,6},{6,7},{8,9},{9,10},{10,11},{11... | collective-permute-start | bytes 392 | tf_op jit(solution)/shard_map/ppermute | solution.py:27
  9.6 3.8 %collective-permute-start.2 = (s32[2,1,128]{2,1,0:T(1,128)S(1)}, s32[2,1,128]{2,1,0:T(1,128)S(1)}, u32[]{:S(2)}, u32[]{:S(2)}) collective-permute-start(s32[2,1,128]{2,1,0:T(1,128)S(1)} %get-tuple-element.71), channel_id=1, source_target_pairs={{8,0},{16,8},{24,16},{32,24},{40,32},{48,40},{56,48},{9,1},{17,9},... | collective-permute-start | bytes 3080 | tf_op jit(solution)/shard_map/ppermute | solution.py:28
  13.4 1.9 collective-permute-start.1
  15.4 3.7 %copy.347 = f32[24,64,1,1,4,128]{5,0,1,4,3,2:T(8,128)S(1)} copy(f32[24,64,1,1,4,128]{5,4,3,2,1,0:T(4,128)} %param.19) | data formatting | bytes 6291456 | tf_op args[6]
  19.1 3.6 %fusion.72 = (f32[24,64,4,1]{3,0,1,2:T(8,128)}, f32[24,64,4,1]{3,0,1,2:T(8,128)}) fusion(f32[24,64,4,128]{3,0,1,2:T(8,128)S(1)} %bitcast.166), kind=kLoop, calls=%fused_computation.157 | loop fusion | bytes 98304 | tf_op jit(solution)/shard_map/slice | solution.py:71
  22.7 3.1 %copy.252 = f32[24,64,4,1]{1,0,3,2:T(8,128)} copy(f32[24,64,4,1]{3,0,1,2:T(8,128)} %get-tuple-element.54) | data formatting | bytes 49152 | tf_op jit(solution)/shard_map/slice | solution.py:71
  25.8 2.7 %collective-permute-start.15 = (f32[24,64,4,1]{1,0,3,2:T(8,128)}, f32[24,64,4,1]{1,0,3,2:T(8,128)}, u32[]{:S(2)}, u32[]{:S(2)}) collective-permute-start(f32[24,64,4,1]{1,0,3,2:T(8,128)} %copy.252), channel_id=1, source_target_pairs={{0,1},{1,2},{2,3},{3,4},{4,5},{5,6},{6,7},{8,9},{9,10},{10,11},{11... | collective-permute-start | bytes 73736 | tf_op jit(solution)/shard_map/ppermute | solution.py:74
  28.5 1.3 slice_bitcast_fusion.3
  30.9 3.1 %copy.255 = f32[24,64,4,1]{1,0,3,2:T(8,128)} copy(f32[24,64,4,1]{3,0,1,2:T(8,128)} %get-tuple-element.55) | data formatting | bytes 49152 | tf_op jit(solution)/shard_map/slice | solution.py:70
  34.0 2.2 collective-permute-start.16
  37.2 1.7 fusion.70
  39.5 4.3 %all-to-all-start = ((f32[4,1,16,128]{3,2,1,0:T(8,128)}), f32[4,1,16,128]{3,2,1,0:T(8,128)S(1)}, u32[]{:S(2)}, u32[]{:S(2)}) async-start(f32[4,1,16,128]{3,2,1,0:T(8,128)} %broadcast_in_dim.10), calls=%async_computation | async-start | bytes 65536 | tf_op jit(solution)/shard_map/all_to_all | solution.py:41
  43.9 1.9 slice_multiply_fusion
  45.8 1.3 all-to-all-done
  47.8 1.2 fusion.26
  50.0 2.7 %collective-permute-start.6 = (f32[3,16,16,1]{3,1,2,0:T(8,128)S(1)}, f32[3,16,16,1]{3,1,2,0:T(8,128)S(1)}, u32[]{:S(2)}, u32[]{:S(2)}) collective-permute-start(f32[3,16,16,1]{3,1,2,0:T(8,128)S(1)} %get-tuple-element.57), channel_id=1, source_target_pairs={{1,0},{2,1},{3,2},{4,3},{5,4},{6,5},{7,6},{9,8},{10,9},{11,10},{12... | collective-permute-start | bytes 9224 | tf_op jit(solution)/shard_map/ppermute | solution.py:28
  52.7 4.3 %collective-permute-start.4 = (f32[3,16,1,128]{3,1,2,0:T(8,128)S(1)}, f32[3,16,1,128]{3,1,2,0:T(8,128)S(1)}, u32[]{:S(2)}, u32[]{:S(2)}) collective-permute-start(f32[3,16,1,128]{3,1,2,0:T(8,128)S(1)} %get-tuple-element.61), channel_id=1, source_target_pairs={{8,0},{16,8},{24,16},{32,24},{40,32},{48,40},{56,48},{9,1},{17,9},... | collective-permute-start | bytes 73736 | tf_op jit(solution)/shard_map/ppermute | solution.py:28
  57.0 1.9 collective-permute-start.5
  59.1 6.0 %collective-permute-done.6 = f32[3,16,16,1]{3,1,2,0:T(8,128)S(1)} collective-permute-done((f32[3,16,16,1]{3,1,2,0:T(8,128)S(1)}, f32[3,16,16,1]{3,1,2,0:T(8,128)S(1)}, u32[]{:S(2)}, u32[]{:S(2)}) %collective-permute-start.6) | collective-permute-done | bytes 3104 | tf_op jit(solution)/shard_map/ppermute | solution.py:28
  65.1 1.6 collective-permute-start.12
  67.8 1.8 fusion.48
  69.6 5.4 %all-to-all-start.2 = ((f32[16,16,128]{2,0,1:T(8,128)}), f32[16,16,128]{2,0,1:T(8,128)}, u32[]{:S(2)}, u32[]{:S(2)}) async-start(f32[16,16,128]{2,0,1:T(8,128)} %get-tuple-element.58), calls=%async_computation.2 | async-start | bytes 262144 | tf_op jit(solution)/shard_map/all_to_all | solution.py:141
  75.0 1.3 fusion.56
  76.3 5.4 %copy.346 = f32[24,64,1,1,4,128]{5,0,4,1,2,3:T(8,128)} copy(f32[24,64,1,1,4,128]{5,4,3,2,1,0:T(4,128)} %param.19) | data formatting | bytes 6291456 | tf_op jit(solution)/shard_map/reshape | solution.py:168
  81.7 1.7 copy.242
  83.4 3.0 %copy.253 = f32[24,64,4,1]{3,0,1,2:T(8,128)} copy(f32[24,64,4,1]{1,0,3,2:T(8,128)} %collective-permute-done.15) | data formatting | bytes 49152 | tf_op jit(solution)/shard_map/ppermute | solution.py:74
  86.4 3.0 %copy.256 = f32[24,64,4,1]{3,0,1,2:T(8,128)} copy(f32[24,64,4,1]{1,0,3,2:T(8,128)} %collective-permute-done.16) | data formatting | bytes 49152 | tf_op jit(solution)/shard_map/ppermute | solution.py:76
  89.3 4.2 %all-to-all-start.1 = ((f32[16,16,128]{2,0,1:T(8,128)}), f32[16,16,128]{2,0,1:T(8,128)}, u32[]{:S(2)}, u32[]{:S(2)}) async-start(f32[16,16,128]{2,0,1:T(8,128)} %get-tuple-element.59), calls=%async_computation.1 | async-start | bytes 262144 | tf_op jit(solution)/shard_map/all_to_all | solution.py:140
  96.0 3.2 %collective-permute-start.14 = (f32[64,4]{0,1:T(4,128)}, f32[64,4]{0,1:T(4,128)}, u32[]{:S(2)}, u32[]{:S(2)}) collective-permute-start(f32[64,4]{0,1:T(4,128)} %slice_reduce_fusion), channel_id=1, source_target_pairs={{0,1},{1,2},{2,3},{3,4},{4,5},{5,6},{6,7},{8,9},{9,10},{10,11},{11... | collective-permute-start | bytes 3080 | tf_op jit(solution)/shard_map/ppermute | solution.py:58
  101.4 1.2 collective-permute-start.8
  102.6 1.4 copy.250
  104.0 1.1 fusion.36
  105.2 4.7 %pad_maximum_fusion = (f32[24,64,4,129]{3,0,1,2:T(8,128)S(1)}, f32[24,64,4,129]{3,0,1,2:T(8,128)S(1)}) fusion(f32[24,64,4,128]{3,0,1,2:T(8,128)S(1)} %bitcast.168, f32[24,64,4,1]{3,0,1,2:T(8,128)} %copy.253, f32[24,64,4,1]{3,0,1,2:T(8,128)} %copy.256, f32[64,4,129]{2,0,1:T(8,128)S(1)} %get-tuple-element.65), kind=kLoop, calls=%fused_computation | loop fusion | flops 2377728 | bytes 9667584 | tf_op jit(solution)/shard_map/concatenate | solution.py:72
  110.8 1.9 collective-permute-start.9
  112.7 4.3 %collective-permute-start.13 = (f32[24,64,128]{2,0,1:T(8,128)}, f32[24,64,128]{2,0,1:T(8,128)}, u32[]{:S(2)}, u32[]{:S(2)}) collective-permute-start(f32[24,64,128]{2,0,1:T(8,128)} %collective-permute-done.12), channel_id=1, source_target_pairs={{8,0},{16,8},{24,16},{32,24},{40,32},{48,40},{56,48},{9,1},{17,9},... | collective-permute-start | bytes 2359304 | tf_op jit(solution)/shard_map/ppermute | solution.py:58
  117.0 2.0 collective-permute-start.11
  118.9 4.6 %copy_add_fusion = f32[24,64,4,129]{3,0,2,1:T(8,128)} fusion(f32[24,64,4,129]{3,0,1,2:T(8,128)S(1)} %get-tuple-element.53, f32[24,64,4,129]{3,0,1,2:T(8,128)S(1)} %get-tuple-element.52, f32[64,4,129]{2,1,0:T(4,128)} %copy.251), kind=kLoop, calls=%fused_computation.5 | loop fusion | flops 1585152 | bytes 9643008 | tf_op jit(solution)/shard_map/add | solution.py:184
  126.1 25.4 %collective-permute-done.11 = f32[24,64,128]{2,0,1:T(8,128)} collective-permute-done((f32[24,64,128]{2,0,1:T(8,128)}, f32[24,64,128]{2,0,1:T(8,128)}, u32[]{:S(2)}, u32[]{:S(2)}) %collective-permute-start.11) | collective-permute-done | bytes 786464 | tf_op jit(solution)/shard_map/ppermute | solution.py:58
  151.4 1.2 select_bitcast_fusion.3
  152.7 1.2 select_bitcast_fusion.2
  155.8 6.8 %fusion.7 = f32[24,64,4,128]{3,0,2,1:T(8,128)S(1)} fusion(f32[24,64,4,129]{3,0,2,1:T(8,128)} %copy_add_fusion, f32[24,64,5,128]{3,0,2,1:T(8,128)S(1)} %fusion.1, f32[64,4,128]{2,1,0:T(4,128)} %copy.242, f32[24,64,1,1,4,128]{5,4,3,2,1,0:T(4,128)S(1)} %copy-done.1), kind=kLoop, calls=%fused_computation.20 | loop fusion | flops 3932160 | bytes 19005440 | tf_op jit(solution)/shard_map/mul | solution.py:188
  164.5 8.6 %collective-permute-start.7 = (f32[3,16,16,1]{3,1,2,0:T(8,128)S(1)}, f32[3,16,16,1]{3,1,2,0:T(8,128)S(1)}, u32[]{:S(2)}, u32[]{:S(2)}) collective-permute-start(f32[3,16,16,1]{3,1,2,0:T(8,128)S(1)} %copy-done.24), channel_id=1, source_target_pairs={{0,1},{1,2},{2,3},{3,4},{4,5},{5,6},{6,7},{8,9},{9,10},{10,11},{11... | collective-permute-start | bytes 9224 | tf_op jit(solution)/shard_map/ppermute | solution.py:27
  173.1 4.7 %collective-permute-done.7 = f32[3,16,16,1]{3,1,2,0:T(8,128)S(1)} collective-permute-done((f32[3,16,16,1]{3,1,2,0:T(8,128)S(1)}, f32[3,16,16,1]{3,1,2,0:T(8,128)S(1)}, u32[]{:S(2)}, u32[]{:S(2)}) %collective-permute-start.7) | collective-permute-done | bytes 3104 | tf_op jit(solution)/shard_map/ppermute | solution.py:27
  179.6 2.1 collective-permute-done.17
  181.7 3.4 %collective-permute-start.18 = (f32[24,64,128]{2,0,1:T(8,128)}, f32[24,64,128]{2,0,1:T(8,128)}, u32[]{:S(2)}, u32[]{:S(2)}) collective-permute-start(f32[24,64,128]{2,0,1:T(8,128)} %collective-permute-done.17), channel_id=1, source_target_pairs={{0,8},{8,16},{16,24},{24,32},{32,40},{40,48},{48,56},{1,9},{9,17},... | collective-permute-start | bytes 2359304 | tf_op jit(solution)/shard_map/ppermute | solution.py:58
  185.1 3.8 %fusion.71 = (f32[24,64,4,1]{3,0,2,1:T(8,128)}, f32[24,64,4,1]{3,0,2,1:T(8,128)}) fusion(f32[24,64,4,128]{3,0,2,1:T(8,128)S(1)} %fusion.7), kind=kLoop, calls=%fused_computation.156 | loop fusion | bytes 98304 | tf_op jit(solution)/shard_map/slice | solution.py:70
  188.9 3.3 %copy.263 = f32[24,64,4,1]{1,0,3,2:T(8,128)} copy(f32[24,64,4,1]{3,0,2,1:T(8,128)} %get-tuple-element.49) | data formatting | bytes 49152 | tf_op jit(solution)/shard_map/slice | solution.py:71
  192.2 8.4 %collective-permute-start.21 = (f32[24,64,4,1]{1,0,3,2:T(8,128)}, f32[24,64,4,1]{1,0,3,2:T(8,128)}, u32[]{:S(2)}, u32[]{:S(2)}) collective-permute-start(f32[24,64,4,1]{1,0,3,2:T(8,128)} %copy.263), channel_id=1, source_target_pairs={{0,1},{1,2},{2,3},{3,4},{4,5},{5,6},{6,7},{8,9},{9,10},{10,11},{11... | collective-permute-start | bytes 73736 | tf_op jit(solution)/shard_map/ppermute | solution.py:74
  200.5 3.2 %copy.265 = f32[24,64,4,1]{1,0,3,2:T(8,128)} copy(f32[24,64,4,1]{3,0,2,1:T(8,128)} %get-tuple-element.48) | data formatting | bytes 49152 | tf_op jit(solution)/shard_map/slice | solution.py:70
  203.8 1.9 collective-permute-start.22
  205.7 4.8 %collective-permute-start.20 = (f32[24,64,128]{2,0,1:T(8,128)}, f32[24,64,128]{2,0,1:T(8,128)}, u32[]{:S(2)}, u32[]{:S(2)}) collective-permute-start(f32[24,64,128]{2,0,1:T(8,128)} %collective-permute-done.19), channel_id=1, source_target_pairs={{8,0},{16,8},{24,16},{32,24},{40,32},{48,40},{56,48},{9,1},{17,9},... | collective-permute-start | bytes 2359304 | tf_op jit(solution)/shard_map/ppermute | solution.py:58
  211.4 1.6 copy.276
  215.3 3.2 %copy.264 = f32[24,64,4,1]{3,0,2,1:T(8,128)} copy(f32[24,64,4,1]{1,0,3,2:T(8,128)} %collective-permute-done.21) | data formatting | bytes 49152 | tf_op jit(solution)/shard_map/ppermute | solution.py:74
  218.5 3.2 %copy.266 = f32[24,64,4,1]{3,0,2,1:T(8,128)} copy(f32[24,64,4,1]{1,0,3,2:T(8,128)} %collective-permute-done.22) | data formatting | bytes 49152 | tf_op jit(solution)/shard_map/ppermute | solution.py:76
  221.6 4.3 %fusion = f32[24,64,4,129]{3,0,2,1:T(8,128)S(1)} fusion(f32[24,64,4,128]{3,0,2,1:T(8,128)S(1)} %fusion.7, f32[24,64,4,1]{3,0,2,1:T(8,128)} %copy.264, f32[24,64,4,1]{3,0,2,1:T(8,128)} %copy.266, f32[64,4,129]{2,1,0:T(4,128)} %copy.288, f32[64,4,129]{2,1,0:T(4,128)S(1)} %copy-done.8), kind=kLoop, calls=%fused_computation.3 | loop fusion | flops 3962880 | bytes 6629376 | tf_op jit(solution)/shard_map/add | solution.py:184
  226.0 1.3 select_bitcast_fusion.1
  227.3 1.2 select_bitcast_fusion
  229.6 1.4 fusion.4
  231.1 1.6 copy-done.2
  232.7 1.7 fusion.67
  235.4 4.8 %all-to-all-start.3 = ((f32[64,4,128]{2,1,0:T(4,128)}), f32[64,4,128]{2,1,0:T(4,128)S(1)}, u32[]{:S(2)}, u32[]{:S(2)}) async-start(f32[64,4,128]{2,1,0:T(4,128)} %copy.271), calls=%async_computation.3 | async-start | bytes 262144 | tf_op jit(solution)/shard_map/all_to_all | solution.py:204
  240.4 7.0 %fusion.9 = f32[24,64,1,1,4,128]{5,0,4,1,3,2:T(8,128)S(1)} fusion(f32[24,64,4,128]{3,0,2,1:T(8,128)} %copy-done.2, f32[24]{0:T(128)} %param.24, f32[64,4,128]{2,1,0:T(4,128)S(1)} %copy.275, f32[24]{0:T(128)} %param.23, f32[64,4,128]{2,1,0:T(4,128)S(1)} %bitcast.184, f32[24]{0:T(128)} %param.22, f32[64,4,128]{2,1,0:T(4,128)S(1)} %copy.274, ...), kind=kOutput, calls=%fused_computation.24 | convolution fusion | flops 233570304 | bytes 6687264 | tf_op jit(solution)/shard_map/dot_general | solution.py:212
  247.4 2.5 copy.281
  (141 shorter events, 28.7 us)
Async XLA Ops:
  0.6 239.7 %copy-start = (f32[24,24]{1,0:T(8,128)S(1)}, f32[24,24]{1,0:T(8,128)}, u32[]{:S(2)}) copy-start(f32[24,24]{1,0:T(8,128)} %param.25) | copy-start | bytes 6916
  1.5 32.5 %collective-permute-start.3 = (s32[2,16,1]{2,1,0:T(8,128)S(1)}, s32[2,16,1]{2,1,0:T(8,128)S(1)}, u32[]{:S(2)}, u32[]{:S(2)}) collective-permute-start(s32[2,16,1]{2,1,0:T(8,128)S(1)} %get-tuple-element.73), channel_id=1, source_target_pairs={{1,0},{2,1},{3,2},{4,3},{5,4},{6,5},{7,6},{9,8},{10,9},{11,10},{12... | collective-permute-start | bytes 392 | tf_op jit(solution)/shard_map/ppermute | solution.py:28
  4.1 32.1 %collective-permute-start = (s32[2,16,1]{2,1,0:T(8,128)S(1)}, s32[2,16,1]{2,1,0:T(8,128)S(1)}, u32[]{:S(2)}, u32[]{:S(2)}) collective-permute-start(s32[2,16,1]{2,1,0:T(8,128)S(1)} %get-tuple-element.72), channel_id=1, source_target_pairs={{0,1},{1,2},{2,3},{3,4},{4,5},{5,6},{6,7},{8,9},{9,10},{10,11},{11... | collective-permute-start | bytes 392 | tf_op jit(solution)/shard_map/ppermute | solution.py:27
  9.6 26.6 %collective-permute-start.2 = (s32[2,1,128]{2,1,0:T(1,128)S(1)}, s32[2,1,128]{2,1,0:T(1,128)S(1)}, u32[]{:S(2)}, u32[]{:S(2)}) collective-permute-start(s32[2,1,128]{2,1,0:T(1,128)S(1)} %get-tuple-element.71), channel_id=1, source_target_pairs={{8,0},{16,8},{24,16},{32,24},{40,32},{48,40},{56,48},{9,1},{17,9},... | collective-permute-start | bytes 3080 | tf_op jit(solution)/shard_map/ppermute | solution.py:28
  13.4 22.8 %collective-permute-start.1 = (s32[2,1,128]{2,1,0:T(1,128)S(1)}, s32[2,1,128]{2,1,0:T(1,128)S(1)}, u32[]{:S(2)}, u32[]{:S(2)}) collective-permute-start(s32[2,1,128]{2,1,0:T(1,128)S(1)} %get-tuple-element.70), channel_id=1, source_target_pairs={{0,8},{8,16},{16,24},{24,32},{32,40},{40,48},{48,56},{1,9},{9,17},... | collective-permute-start | bytes 3080 | tf_op jit(solution)/shard_map/ppermute | solution.py:27
  22.7 7.6 %copy-start.31 = (s32[16,128]{1,0:T(8,128)S(1)}, s32[16,128]{1,0:T(8,128)}, u32[]{:S(2)}) copy-start(s32[16,128]{1,0:T(8,128)} %param.18) | copy-start | bytes 24580
  22.7 7.6 %copy-start.30 = (s32[16,128]{1,0:T(8,128)S(1)}, s32[16,128]{1,0:T(8,128)}, u32[]{:S(2)}) copy-start(s32[16,128]{1,0:T(8,128)} %param.17) | copy-start | bytes 24580
  25.8 57.5 %collective-permute-start.15 = (f32[24,64,4,1]{1,0,3,2:T(8,128)}, f32[24,64,4,1]{1,0,3,2:T(8,128)}, u32[]{:S(2)}, u32[]{:S(2)}) collective-permute-start(f32[24,64,4,1]{1,0,3,2:T(8,128)} %copy.252), channel_id=1, source_target_pairs={{0,1},{1,2},{2,3},{3,4},{4,5},{5,6},{6,7},{8,9},{9,10},{10,11},{11... | collective-permute-start | bytes 73736 | tf_op jit(solution)/shard_map/ppermute | solution.py:74
  28.5 8.7 %copy-start.29 = (f32[16,16,128]{2,1,0:T(8,128)S(1)}, f32[16,16,128]{2,1,0:T(8,128)}, u32[]{:S(2)}) copy-start(f32[16,16,128]{2,1,0:T(8,128)} %param.16) | copy-start | bytes 393220
  34.0 52.4 %collective-permute-start.16 = (f32[24,64,4,1]{1,0,3,2:T(8,128)}, f32[24,64,4,1]{1,0,3,2:T(8,128)}, u32[]{:S(2)}, u32[]{:S(2)}) collective-permute-start(f32[24,64,4,1]{1,0,3,2:T(8,128)} %copy.255), channel_id=1, source_target_pairs={{1,0},{2,1},{3,2},{4,3},{5,4},{6,5},{7,6},{9,8},{10,9},{11,10},{12... | collective-permute-start | bytes 73736 | tf_op jit(solution)/shard_map/ppermute | solution.py:76
  36.5 0.7 copy-start.4
  39.5 7.5 %all-to-all-start = ((f32[4,1,16,128]{3,2,1,0:T(8,128)}), f32[4,1,16,128]{3,2,1,0:T(8,128)S(1)}, u32[]{:S(2)}, u32[]{:S(2)}) async-start(f32[4,1,16,128]{3,2,1,0:T(8,128)} %broadcast_in_dim.10), calls=%async_computation | async-start | bytes 65536 | tf_op jit(solution)/shard_map/all_to_all | solution.py:41
  47.0 11.9 %copy-start.5 = (f32[16,18,130]{2,0,1:T(8,128)S(1)}, f32[16,18,130]{2,0,1:T(8,128)}, u32[]{:S(2)}) copy-start(f32[16,18,130]{2,0,1:T(8,128)} %copy-done.4) | copy-start | bytes 449284
  47.1 20.7 %copy-start.12 = (f32[16,16,129]{2,0,1:T(8,128)S(1)}, f32[16,16,129]{2,0,1:T(8,128)}, u32[]{:S(2)}) copy-start(f32[16,16,129]{2,0,1:T(8,128)} %slice_multiply_fusion) | copy-start | bytes 396292
  50.0 15.1 %collective-permute-start.6 = (f32[3,16,16,1]{3,1,2,0:T(8,128)S(1)}, f32[3,16,16,1]{3,1,2,0:T(8,128)S(1)}, u32[]{:S(2)}, u32[]{:S(2)}) collective-permute-start(f32[3,16,16,1]{3,1,2,0:T(8,128)S(1)} %get-tuple-element.57), channel_id=1, source_target_pairs={{1,0},{2,1},{3,2},{4,3},{5,4},{6,5},{7,6},{9,8},{10,9},{11,10},{12... | collective-permute-start | bytes 9224 | tf_op jit(solution)/shard_map/ppermute | solution.py:28
  52.7 14.0 %collective-permute-start.4 = (f32[3,16,1,128]{3,1,2,0:T(8,128)S(1)}, f32[3,16,1,128]{3,1,2,0:T(8,128)S(1)}, u32[]{:S(2)}, u32[]{:S(2)}) collective-permute-start(f32[3,16,1,128]{3,1,2,0:T(8,128)S(1)} %get-tuple-element.61), channel_id=1, source_target_pairs={{8,0},{16,8},{24,16},{32,24},{40,32},{48,40},{56,48},{9,1},{17,9},... | collective-permute-start | bytes 73736 | tf_op jit(solution)/shard_map/ppermute | solution.py:28
  57.0 9.7 %collective-permute-start.5 = (f32[3,16,1,128]{3,1,2,0:T(8,128)S(1)}, f32[3,16,1,128]{3,1,2,0:T(8,128)S(1)}, u32[]{:S(2)}, u32[]{:S(2)}) collective-permute-start(f32[3,16,1,128]{3,1,2,0:T(8,128)S(1)} %get-tuple-element.60), channel_id=1, source_target_pairs={{0,8},{8,16},{16,24},{24,32},{32,40},{40,48},{48,56},{1,9},{9,17},... | collective-permute-start | bytes 73736 | tf_op jit(solution)/shard_map/ppermute | solution.py:27
  59.1 10.5 %copy-start.18 = (f32[16,17,128]{2,0,1:T(8,128)}, f32[16,17,128]{2,0,1:T(8,128)S(1)}, u32[]{:S(2)}) copy-start(f32[16,17,128]{2,0,1:T(8,128)S(1)} %slice_multiply_fusion.1) | copy-start | bytes 417796
  65.1 47.6 %collective-permute-start.12 = (f32[24,64,128]{2,0,1:T(8,128)}, f32[24,64,128]{2,0,1:T(8,128)}, u32[]{:S(2)}, u32[]{:S(2)}) collective-permute-start(f32[24,64,128]{2,0,1:T(8,128)} %get-tuple-element.51), channel_id=1, source_target_pairs={{0,192},{64,0},{128,64},{192,128},{1,193},{65,1},{129,65},{193,129... | collective-permute-start | bytes 2359304 | tf_op jit(solution)/shard_map/ppermute | solution.py:63
  66.7 2.9 %copy-start.25 = (f32[3,16,1,128]{3,1,2,0:T(8,128)}, f32[3,16,1,128]{3,1,2,0:T(8,128)S(1)}, u32[]{:S(2)}) copy-start(f32[3,16,1,128]{3,1,2,0:T(8,128)S(1)} %collective-permute-done.4) | copy-start | bytes 73732
  66.7 50.2 %collective-permute-start.10 = (f32[24,64,128]{2,0,1:T(8,128)}, f32[24,64,128]{2,0,1:T(8,128)}, u32[]{:S(2)}, u32[]{:S(2)}) collective-permute-start(f32[24,64,128]{2,0,1:T(8,128)} %get-tuple-element.50), channel_id=1, source_target_pairs={{0,64},{64,128},{128,192},{192,0},{1,65},{65,129},{129,193},{193,1... | collective-permute-start | bytes 2359304 | tf_op jit(solution)/shard_map/ppermute | solution.py:63
  66.7 2.9 %copy-start.27 = (f32[3,16,1,128]{3,1,2,0:T(8,128)}, f32[3,16,1,128]{3,1,2,0:T(8,128)S(1)}, u32[]{:S(2)}) copy-start(f32[3,16,1,128]{3,1,2,0:T(8,128)S(1)} %collective-permute-done.5) | copy-start | bytes 73732
  66.8 0.9 copy-start.6
  69.6 19.7 %all-to-all-start.2 = ((f32[16,16,128]{2,0,1:T(8,128)}), f32[16,16,128]{2,0,1:T(8,128)}, u32[]{:S(2)}, u32[]{:S(2)}) async-start(f32[16,16,128]{2,0,1:T(8,128)} %get-tuple-element.58), calls=%async_computation.2 | async-start | bytes 262144 | tf_op jit(solution)/shard_map/all_to_all | solution.py:141
  89.3 9.9 %all-to-all-start.1 = ((f32[16,16,128]{2,0,1:T(8,128)}), f32[16,16,128]{2,0,1:T(8,128)}, u32[]{:S(2)}, u32[]{:S(2)}) async-start(f32[16,16,128]{2,0,1:T(8,128)} %get-tuple-element.59), calls=%async_computation.1 | async-start | bytes 262144 | tf_op jit(solution)/shard_map/all_to_all | solution.py:140
  94.5 0.7 copy-start.22
  96.0 6.6 %collective-permute-start.14 = (f32[64,4]{0,1:T(4,128)}, f32[64,4]{0,1:T(4,128)}, u32[]{:S(2)}, u32[]{:S(2)}) collective-permute-start(f32[64,4]{0,1:T(4,128)} %slice_reduce_fusion), channel_id=1, source_target_pairs={{0,1},{1,2},{2,3},{3,4},{4,5},{5,6},{6,7},{8,9},{9,10},{10,11},{11... | collective-permute-start | bytes 3080 | tf_op jit(solution)/shard_map/ppermute | solution.py:58
  100.2 0.7 copy-start.23
  101.4 9.3 %collective-permute-start.8 = (f32[64,128]{1,0:T(8,128)}, f32[64,128]{1,0:T(8,128)}, u32[]{:S(2)}, u32[]{:S(2)}) collective-permute-start(f32[64,128]{1,0:T(8,128)} %slice_bitcast_fusion.7), channel_id=1, source_target_pairs={{0,64},{64,128},{128,192},{192,0},{1,65},{65,129},{129,193},{193,1... | collective-permute-start | bytes 98312 | tf_op jit(solution)/shard_map/ppermute | solution.py:63
  105.2 4.7 %copy-start.9 = (f32[64,4,129]{2,0,1:T(8,128)}, f32[64,4,129]{2,0,1:T(8,128)S(1)}, u32[]{:S(2)}) copy-start(f32[64,4,129]{2,0,1:T(8,128)S(1)} %get-tuple-element.65) | copy-start | bytes 396292
  110.8 12.8 %collective-permute-start.9 = (f32[64,128]{1,0:T(8,128)}, f32[64,128]{1,0:T(8,128)S(1)}, u32[]{:S(2)}, u32[]{:S(2)}) collective-permute-start(f32[64,128]{1,0:T(8,128)} %collective-permute-done.8), channel_id=1, source_target_pairs={{0,8},{8,16},{16,24},{24,32},{32,40},{40,48},{48,56},{1,9},{9,17},... | collective-permute-start | bytes 98312 | tf_op jit(solution)/shard_map/ppermute | solution.py:58
  112.7 40.0 %collective-permute-start.13 = (f32[24,64,128]{2,0,1:T(8,128)}, f32[24,64,128]{2,0,1:T(8,128)}, u32[]{:S(2)}, u32[]{:S(2)}) collective-permute-start(f32[24,64,128]{2,0,1:T(8,128)} %collective-permute-done.12), channel_id=1, source_target_pairs={{8,0},{16,8},{24,16},{32,24},{40,32},{48,40},{56,48},{9,1},{17,9},... | collective-permute-start | bytes 2359304 | tf_op jit(solution)/shard_map/ppermute | solution.py:58
  117.0 34.5 %collective-permute-start.11 = (f32[24,64,128]{2,0,1:T(8,128)}, f32[24,64,128]{2,0,1:T(8,128)}, u32[]{:S(2)}, u32[]{:S(2)}) collective-permute-start(f32[24,64,128]{2,0,1:T(8,128)} %collective-permute-done.10), channel_id=1, source_target_pairs={{0,8},{8,16},{16,24},{24,32},{32,40},{40,48},{48,56},{1,9},{9,17},... | collective-permute-start | bytes 2359304 | tf_op jit(solution)/shard_map/ppermute | solution.py:58
  123.5 30.4 %copy-start.3 = (f32[24,64,1,1,4,128]{5,0,4,1,2,3:T(8,128)S(1)}, f32[24,64,1,1,4,128]{5,0,4,1,2,3:T(8,128)}, u32[]{:S(2)}) copy-start(f32[24,64,1,1,4,128]{5,0,4,1,2,3:T(8,128)} %copy.346) | copy-start | bytes 9437188
  125.4 0.7 copy-start.14
  125.4 28.5 %copy-start.16 = (f32[64,5,128]{2,0,1:T(8,128)}, f32[64,5,128]{2,0,1:T(8,128)S(1)}, u32[]{:S(2)}) copy-start(f32[64,5,128]{2,0,1:T(8,128)S(1)} %get-tuple-element.67) | copy-start | bytes 491524
  153.9 1.9 copy-start.1
  162.6 2.0 copy-start.24
  162.6 15.3 %copy-start.7 = (f32[3,16,18,129]{3,1,2,0:T(8,128)S(1)}, f32[3,16,18,129]{3,1,2,0:T(8,128)}, u32[]{:S(2)}) copy-start(f32[3,16,18,129]{3,1,2,0:T(8,128)} %copy-done.6) | copy-start | bytes 1337476
  162.6 15.3 %copy-start.13 = (f32[16,16,129]{2,0,1:T(8,128)S(1)}, f32[16,16,129]{2,0,1:T(8,128)}, u32[]{:S(2)}) copy-start(f32[16,16,129]{2,0,1:T(8,128)} %slice_multiply_fusion) | copy-start | bytes 396292
  162.6 15.3 %copy-start.26 = (f32[3,16,1,128]{3,1,2,0:T(8,128)S(1)}, f32[3,16,1,128]{3,1,2,0:T(8,128)}, u32[]{:S(2)}) copy-start(f32[3,16,1,128]{3,1,2,0:T(8,128)} %copy-done.25) | copy-start | bytes 73732
  162.6 15.2 %copy-start.28 = (f32[3,16,1,128]{3,1,2,0:T(8,128)S(1)}, f32[3,16,1,128]{3,1,2,0:T(8,128)}, u32[]{:S(2)}) copy-start(f32[3,16,1,128]{3,1,2,0:T(8,128)} %copy-done.27) | copy-start | bytes 73732
  162.6 16.1 %copy-start.19 = (f32[16,17,128]{2,0,1:T(8,128)S(1)}, f32[16,17,128]{2,0,1:T(8,128)}, u32[]{:S(2)}) copy-start(f32[16,17,128]{2,0,1:T(8,128)} %copy-done.18) | copy-start | bytes 417796
  163.6 18.1 %collective-permute-start.17 = (f32[24,64,128]{2,0,1:T(8,128)S(1)}, f32[24,64,128]{2,0,1:T(8,128)}, u32[]{:S(2)}, u32[]{:S(2)}) collective-permute-start(f32[24,64,128]{2,0,1:T(8,128)S(1)} %get-tuple-element.47), channel_id=1, source_target_pairs={{0,64},{64,128},{128,192},{192,0},{1,65},{65,129},{129,193},{193,1... | collective-permute-start | bytes 2359304 | tf_op jit(solution)/shard_map/ppermute | solution.py:63
  164.5 13.3 %collective-permute-start.7 = (f32[3,16,16,1]{3,1,2,0:T(8,128)S(1)}, f32[3,16,16,1]{3,1,2,0:T(8,128)S(1)}, u32[]{:S(2)}, u32[]{:S(2)}) collective-permute-start(f32[3,16,16,1]{3,1,2,0:T(8,128)S(1)} %copy-done.24), channel_id=1, source_target_pairs={{0,1},{1,2},{2,3},{3,4},{4,5},{5,6},{6,7},{8,9},{9,10},{10,11},{11... | collective-permute-start | bytes 9224 | tf_op jit(solution)/shard_map/ppermute | solution.py:27
  178.1 27.6 %collective-permute-start.19 = (f32[24,64,128]{2,0,1:T(8,128)}, f32[24,64,128]{2,0,1:T(8,128)}, u32[]{:S(2)}, u32[]{:S(2)}) collective-permute-start(f32[24,64,128]{2,0,1:T(8,128)} %get-tuple-element.46), channel_id=1, source_target_pairs={{0,192},{64,0},{128,64},{192,128},{1,193},{65,1},{129,65},{193,129... | collective-permute-start | bytes 2359304 | tf_op jit(solution)/shard_map/ppermute | solution.py:63
  181.7 44.3 %collective-permute-start.18 = (f32[24,64,128]{2,0,1:T(8,128)}, f32[24,64,128]{2,0,1:T(8,128)}, u32[]{:S(2)}, u32[]{:S(2)}) collective-permute-start(f32[24,64,128]{2,0,1:T(8,128)} %collective-permute-done.17), channel_id=1, source_target_pairs={{0,8},{8,16},{16,24},{24,32},{32,40},{40,48},{48,56},{1,9},{9,17},... | collective-permute-start | bytes 2359304 | tf_op jit(solution)/shard_map/ppermute | solution.py:58
  188.9 24.1 %copy-start.21 = (f32[16,16,128]{2,0,1:T(8,128)S(1)}, f32[16,16,128]{2,0,1:T(8,128)}, u32[]{:S(2)}) copy-start(f32[16,16,128]{2,0,1:T(8,128)} %get-tuple-element.58) | copy-start | bytes 393220
  188.9 25.5 %copy-start.10 = (f32[64,4,129]{2,0,1:T(8,128)S(1)}, f32[64,4,129]{2,0,1:T(8,128)}, u32[]{:S(2)}) copy-start(f32[64,4,129]{2,0,1:T(8,128)} %copy-done.9) | copy-start | bytes 396292
  192.2 23.1 %collective-permute-start.21 = (f32[24,64,4,1]{1,0,3,2:T(8,128)}, f32[24,64,4,1]{1,0,3,2:T(8,128)}, u32[]{:S(2)}, u32[]{:S(2)}) collective-permute-start(f32[24,64,4,1]{1,0,3,2:T(8,128)} %copy.263), channel_id=1, source_target_pairs={{0,1},{1,2},{2,3},{3,4},{4,5},{5,6},{6,7},{8,9},{9,10},{10,11},{11... | collective-permute-start | bytes 73736 | tf_op jit(solution)/shard_map/ppermute | solution.py:74
  203.8 14.7 %collective-permute-start.22 = (f32[24,64,4,1]{1,0,3,2:T(8,128)}, f32[24,64,4,1]{1,0,3,2:T(8,128)}, u32[]{:S(2)}, u32[]{:S(2)}) collective-permute-start(f32[24,64,4,1]{1,0,3,2:T(8,128)} %copy.265), channel_id=1, source_target_pairs={{1,0},{2,1},{3,2},{4,3},{5,4},{6,5},{7,6},{9,8},{10,9},{11,10},{12... | collective-permute-start | bytes 73736 | tf_op jit(solution)/shard_map/ppermute | solution.py:76
  205.7 21.6 %collective-permute-start.20 = (f32[24,64,128]{2,0,1:T(8,128)}, f32[24,64,128]{2,0,1:T(8,128)}, u32[]{:S(2)}, u32[]{:S(2)}) collective-permute-start(f32[24,64,128]{2,0,1:T(8,128)} %collective-permute-done.19), channel_id=1, source_target_pairs={{8,0},{16,8},{24,16},{32,24},{40,32},{48,40},{56,48},{9,1},{17,9},... | collective-permute-start | bytes 2359304 | tf_op jit(solution)/shard_map/ppermute | solution.py:58
  215.3 6.4 %copy-start.8 = (f32[64,4,129]{2,1,0:T(4,128)S(1)}, f32[64,4,129]{2,1,0:T(4,128)}, u32[]{:S(2)}) copy-start(f32[64,4,129]{2,1,0:T(4,128)} %copy.251) | copy-start | bytes 396292
  225.9 2.6 %copy-start.15 = (f32[64,5,128]{2,0,1:T(8,128)S(1)}, f32[64,5,128]{2,0,1:T(8,128)}, u32[]{:S(2)}) copy-start(f32[64,5,128]{2,0,1:T(8,128)} %copy-done.14) | copy-start | bytes 491524
  226.0 2.6 %copy-start.17 = (f32[64,5,128]{2,0,1:T(8,128)S(1)}, f32[64,5,128]{2,0,1:T(8,128)}, u32[]{:S(2)}) copy-start(f32[64,5,128]{2,0,1:T(8,128)} %copy-done.16) | copy-start | bytes 491524
  228.5 1.0 copy-start.20
  229.6 3.1 %copy-start.33 = (f32[24]{0:T(128)S(1)}, f32[24]{0:T(128)}, u32[]{:S(2)}) copy-start(f32[24]{0:T(128)} %param.21) | copy-start | bytes 292
  231.0 1.7 copy-start.2
  231.0 3.4 %copy-start.32 = (pred[4,128]{1,0:T(4,128)(4,1)S(1)}, pred[4,128]{1,0:T(4,128)(4,1)}, u32[]{:S(2)}) copy-start(pred[4,128]{1,0:T(4,128)(4,1)} %dynamic-slice_compare_fusion) | copy-start | bytes 1540
  231.0 3.4 %copy-start.34 = (f32[1,1,4,128]{3,2,1,0:T(4,128)S(1)}, f32[1,1,4,128]{3,2,1,0:T(4,128)}, u32[]{:S(2)}) copy-start(f32[1,1,4,128]{3,2,1,0:T(4,128)} %param.20) | copy-start | bytes 6148
  235.4 14.5 %all-to-all-start.3 = ((f32[64,4,128]{2,1,0:T(4,128)}), f32[64,4,128]{2,1,0:T(4,128)S(1)}, u32[]{:S(2)}, u32[]{:S(2)}) async-start(f32[64,4,128]{2,1,0:T(4,128)} %copy.271), calls=%async_computation.3 | async-start | bytes 262144 | tf_op jit(solution)/shard_map/all_to_all | solution.py:204
  247.4 2.5 %copy-start.11 = (f32[2,16,16,128]{3,1,2,0:T(8,128)S(1)}, f32[2,16,16,128]{3,1,2,0:T(8,128)}, u32[]{:S(2)}) copy-start(f32[2,16,16,128]{3,1,2,0:T(8,128)} %fusion.34) | copy-start | bytes 786436
where the time goes:
time: 254 us; the launch traced here: 252 us
  starting transfers between devices  88.2 us (35%)
  local copies, waits for them, and re-layouts  66.7 us (26%)
  other arithmetic  46.3 us (18%)
  waiting for transfers between devices  39.6 us (16%)
  matrix products  10.1 us (4%)
    ppermute x6, waiting for transfers between devices, from_behind(): return lax.ppermute(x, axis, pairs)  25.4 us
    ppermute x6, starting transfers between devices, from_behind(): return lax.ppermute(x, axis, pairs)  19.5 us
    unnamed x79, local copies, waits for them, and re-layouts  17.6 us
    ppermute x4, starting transfers between devices, padded(): lax.ppermute(last, axis, up)  17.2 us
    ppermute x4, starting transfers between devices, padded(): lax.ppermute(first, axis, [(b, a) for a, b in up])  13.3 us
    ppermute x2, starting transfers between devices, extended_2(): lax.ppermute(tail, axis, [(i, (i + 1) % count) for i in range(ends)])  11 us
    slice x3, local copies, waits for them, and re-layouts, extended_2(): head = lax.slice_in_dim(cells, 0, width, axis=dim)  10.1 us
    slice x3, local copies, waits for them, and re-layouts, extended_2(): lax.slice_in_dim(cells, cells.shape[dim] - width, cells.shape[dim], axis=...  10 us
  transfers between devices with their start and end apart: 27, of which 5 were waited for; matrix products, arithmetic and copies ran while one was open for 39% of the time, Pallas kernels for 0%

commit v1 on v0

v1 whole, which is shorter than its diff:
```python
import functools

import jax
import jax.numpy as jnp
from jax import lax
from jax.experimental import pallas as pl
from jax.experimental.pallas import tpu as pltpu
from jax.sharding import PartitionSpec as P

MESH = pl.DeviceIdType.MESH
LANES = 128
GROUP = 8

DT_FLOW = 0.1
CORIOLIS = 0.3
MIXING = 0.15
COURANT = 0.24
DT_BIO = 0.5
WARMING_FACTOR = 0.5
CLEAR_WATER = 0.5


def ocean_kernel(
    dims,
    zonal_ref,
    merid_ref,
    therm_ref,
    brine_ref,
    mask_ref,
    bottom_ref,
    tracer_ref,
    sun_ref,
    absorb_ref,
    growth_ref,
    half_ref,
    light_half_ref,
    stoich_ref,
    east_out,
    north_out,
    warmed_out,
    salt_out,
    buoy_out,
    result_out,
    fld,
    fldh,
    mb,
    mby,
    wet,
    weth,
    den,
    denh,
    tot,
    prs,
    prsh,
    vel,
    cour_e,
    cour_n,
    cour_p,
    cer,
    cnr,
    cpr,
    cps,
    cpack,
    mixed,
    heat,
    fin,
    q0,
    q1,
    res,
    lo,
    hi,
    hsend,
    hrecv,
    coef,
    wcol,
    warm,
    carry,
    upt,
    lsem,
    osem,
    p1s,
    p1r,
    cs_s,
    cs_r,
    ts_s,
    ts_r,
    as_s,
    as_r,
    qs_s,
    qs_r,
    hs_s,
    hs_r,
    ws_s,
    ws_r,
):
    ntr, levels, rows, lev, sub, ng, ny = dims
    nchunk = levels // GROUP
    nc = levels // lev
    c, g, y = lax.axis_index("comp"), lax.axis_index("gx"), lax.axis_index("gy")
    up = {
        "comp": lax.rem(c + 1, nc),
        "gx": jnp.where(c == nc - 1, lax.rem(g + 1, ng), g),
        "gy": y,
    }
    down = {
        "comp": lax.rem(c + nc - 1, nc),
        "gx": jnp.where(c == 0, lax.rem(g + ng - 1, ng), g),
        "gy": y,
    }
    gxp = {"comp": c, "gx": lax.rem(g + 1, ng), "gy": y}
    gxm = {"comp": c, "gx": lax.rem(g + ng - 1, ng), "gy": y}
    gyp = {"comp": c, "gx": g, "gy": lax.rem(y + 1, ny)}
    gym = {"comp": c, "gx": g, "gy": lax.rem(y + ny - 1, ny)}
    peers = [{"comp": lax.rem(c + d, nc), "gx": g, "gy": y} for d in range(1, nc)]

    def remote(src, dst, send, recv, device):
        return pltpu.make_async_remote_copy(
            src_ref=src,
            dst_ref=dst,
            send_sem=send,
            recv_sem=recv,
            device_id=device,
            device_id_type=MESH,
        )

    def chunk(k):
        return pl.ds(pl.multiple_of(k * GROUP, GROUP), GROUP)

    fields = (zonal_ref, merid_ref, therm_ref, brine_ref)

    def load_rows(r, _):
        for f, ref in enumerate(fields):
            pltpu.make_async_copy(ref.at[:, r, 0, :], fld.at[f, r + 1], lsem.at[f]).start()
        return 0

    lax.fori_loop(0, rows, load_rows, 0)
    for i, ref in enumerate((mask_ref, bottom_ref)):
        pltpu.make_async_copy(ref, mb.at[i, pl.ds(1, rows)], lsem.at[4 + i]).start()

    def load_tracers(k, _):
        for r in range(sub):
            pltpu.make_async_copy(
                tracer_ref.at[:, chunk(k), r, 0, :], q0.at[:, r, chunk(k), :], lsem.at[6 + k]
            ).start()
        return 0

    lax.fori_loop(0, nchunk, load_tracers, 0)

    barrier = pltpu.get_barrier_semaphore()
    partners = [up, down, gxp, gxm, gyp, gym] + peers
    for device in partners:
        pl.semaphore_signal(barrier, inc=1, device_id=device, device_id_type=MESH)
    pl.semaphore_wait(barrier, len(partners))

    first = []
    for f, ref in enumerate(fields):
        first.append((ref.at[:, rows - 1, 0, :], fld.at[f, 0], gxp))
    for f in (2, 3):
        first.append((fields[f].at[:, 0, 0, :], fld.at[f, rows + 1], gxm))
    for i, ref in enumerate((mask_ref, bottom_ref)):
        first.append((ref.at[pl.ds(rows - 1, 1)], mb.at[i, pl.ds(0, 1)], gxp))
        first.append((ref.at[pl.ds(0, 1)], mb.at[i, pl.ds(rows + 1, 1)], gxm))
        first.append((ref, mby.at[0, i], gyp))
        first.append((ref, mby.at[1, i], gym))
    first = [
        remote(src, dst, p1s.at[n], p1r.at[n], device)
        for n, (src, dst, device) in enumerate(first)
    ]
    for copy in first:
        copy.start()

    def edge_copies(stage, k):
        if stage == 0:
            top = tracer_ref.at[:, chunk(k), sub - 1, 0, :]
            low = tracer_ref.at[:, chunk(k), 0, 0, :]
        else:
            top = q1.at[:, sub - 1, chunk(k), :]
            low = q1.at[:, 0, chunk(k), :]
        return (
            remote(
                top, lo.at[stage, :, chunk(k), :], qs_s.at[stage, 0, k], qs_r.at[stage, 0, k], up
            ),
            remote(
                low, hi.at[stage, :, chunk(k), :], qs_s.at[stage, 1, k], qs_r.at[stage, 1, k], down
            ),
        )

    def send_edges(stage, k):
        for copy in edge_copies(stage, k):
            copy.start()

    def side_copies(stage, k):
        return (
            remote(
                hsend.at[stage, :, chunk(k), :],
                hrecv.at[stage, 0, :, chunk(k), :],
                hs_s.at[stage, 0, k],
                hs_r.at[stage, 0, k],
                gyp,
            ),
            remote(
                hsend.at[stage, :, chunk(k), :],
                hrecv.at[stage, 1, :, chunk(k), :],
                hs_s.at[stage, 1, k],
                hs_r.at[stage, 1, k],
                gym,
            ),
        )

    def send_sides(stage, k):
        for copy in side_copies(stage, k):
            copy.start()

    send_edges(0, 0)
    send_edges(0, 1)

    lane16 = lax.broadcasted_iota(jnp.int32, (lev, LANES), 1)
    level16 = lax.broadcasted_iota(jnp.int32, (lev, LANES), 0)
    depth16 = (level16 + c * lev).astype(jnp.float32)
    lane8 = lax.broadcasted_iota(jnp.int32, (GROUP, LANES), 1)
    level8 = lax.broadcasted_iota(jnp.int32, (GROUP, LANES), 0)

    def merged(ahead, behind, lanes):
        return jnp.where((lanes & 1) == 1, ahead, pltpu.roll(behind, 2, 1))

    def slot_of(both, m):
        return pltpu.roll(both, (126 - m) % LANES, 1)

    def packed(acc, x, m, lanes):
        return jnp.where((lanes >> 1) == (m >> 1), pltpu.roll(x, (m + 1) % LANES, 1), acc)

    def ahead_of(x, h, lanes):
        return jnp.where(lanes == LANES - 1, h, pltpu.roll(x, LANES - 1, 1))

    def behind_of(x, h, lanes):
        return jnp.where(lanes == 0, h, pltpu.roll(x, 1, 1))

    for f in range(4):
        pltpu.make_async_copy(fld.at[f, pl.ds(1, rows)], fld.at[f, pl.ds(1, rows)], lsem.at[f]).wait()
    acc = jnp.zeros((lev, LANES), jnp.float32)
    for r in range(rows):
        for f in range(4):
            acc = packed(acc, fld[f, r + 1], 8 * r + 2 * f, lane16)
    cps[...] = acc
    column_copies = (
        remote(cps, cpack.at[0], cs_s.at[0], cs_r.at[0], gyp),
        remote(cps, cpack.at[1], cs_s.at[1], cs_r.at[1], gym),
    )
    for copy in column_copies:
        copy.start()

    for i, ref in enumerate((mask_ref, bottom_ref)):
        pltpu.make_async_copy(ref, mb.at[i, pl.ds(1, rows)], lsem.at[4 + i]).wait()

    def reach(m, b):
        return jnp.where(m == 1, b, 0).astype(jnp.float32)

    def wet_row(e, valid):
        depth = reach(mb[0, e], mb[1, e])
        if valid is not None:
            depth = jnp.where(valid, depth, 0.0)
        w = jnp.where(depth16 < depth, 1.0, 0.0)
        d = w * (-0.2 * fld[2, e] + 0.8 * fld[3, e])
        wet[e] = w
        den[e] = d
        tot[c, e] = jnp.sum(d, axis=0, keepdims=True)

    def own_row(r, _):
        wet_row(r + 1, None)
        return 0

    lax.fori_loop(0, rows, own_row, 0)

    def pack_sides(k, _):
        pltpu.make_async_copy(
            q0.at[:, :, chunk(k), :], q0.at[:, :, chunk(k), :], lsem.at[6 + k]
        ).wait()
        for pair in range(sub // 2):
            a = jnp.zeros((GROUP, LANES), jnp.float32)
            for half in range(2):
                for t in range(ntr):
                    a = packed(a, q0[t, 2 * pair + half, chunk(k), :], 64 * half + 2 * t, lane8)
            hsend[0, pair, chunk(k), :] = a
        send_sides(0, k)
        return 0

    lax.fori_loop(0, nchunk, pack_sides, 0)

    for copy in first:
        copy.wait_recv()
    for copy in column_copies:
        copy.wait_recv()
    wet_row(0, g > 0)
    wet_row(rows + 1, g < ng - 1)
    both = merged(cpack[1], cpack[0], lane16)
    for r in range(rows):
        for f in range(4):
            fldh[f, r] = slot_of(both, 8 * r + 2 * f)

    def halo_columns(r, _):
        behind = jnp.broadcast_to(reach(mby[0, 0, r], mby[0, 1, r]), (lev, LANES))
        ahead = jnp.broadcast_to(reach(mby[1, 0, r], mby[1, 1, r]), (lev, LANES))
        behind = jnp.where(y > 0, pltpu.roll(behind, 1, 1), 0.0)
        ahead = jnp.where(y < ny - 1, pltpu.roll(ahead, LANES - 1, 1), 0.0)
        depth = jnp.where(lane16 == 0, behind, ahead)
        w = jnp.where(depth16 < depth, 1.0, 0.0)
        d = w * (-0.2 * fldh[2, r] + 0.8 * fldh[3, r])
        weth[r] = w
        denh[r] = d
        tot[c, rows + 2 + r] = jnp.sum(d, axis=0, keepdims=True)
        return 0

    lax.fori_loop(0, rows, halo_columns, 0)
    total_copies = [
        remote(tot.at[c], tot.at[c], ts_s.at[d], ts_r.at[d], peer) for d, peer in enumerate(peers)
    ]
    for copy in total_copies:
        copy.start()
    send_edges(0, 2)
    send_edges(0, 3)

    def mixing_row(r, _):
        w, h = wet[r + 1], weth[r]
        open_e, open_w = w * wet[r + 2], wet[r] * w
        open_n, open_s = w * ahead_of(w, h, lane16), w * behind_of(w, h, lane16)
        for i in range(2):
            x, xh = fld[2 + i, r + 1], fldh[2 + i, r]
            flux_e = open_e * (fld[2 + i, r + 2] - x)
            flux_w = open_w * (x - fld[2 + i, r])
            flux_n = open_n * (ahead_of(x, xh, lane16) - x)
            flux_s = open_s * (x - behind_of(x, xh, lane16))
            mixed[i, r] = x + MIXING * ((flux_e - flux_w) + (flux_n - flux_s))
        return 0

    lax.fori_loop(0, rows, mixing_row, 0)

    for d, peer in enumerate(peers):
        total_copies[d].wait_recv()

    def pressure_of(d, e):
        incl = d
        step = 1
        while step < lev:
            incl = incl + jnp.where(level16 >= step, pltpu.roll(incl, step, 0), 0.0)
            step *= 2
        offset = jnp.zeros((1, LANES), jnp.float32)
        for p in range(nc - 1):
            offset = offset + jnp.where(p < c, tot[p, e], 0.0)
        return offset + incl - 0.5 * d

    def pressure_row(e, _):
        prs[e] = pressure_of(den[e], e)
        return 0

    def pressure_column(r, _):
        prsh[r] = pressure_of(denh[r], rows + 2 + r)
        return 0

    lax.fori_loop(0, rows + 2, pressure_row, 0)
    lax.fori_loop(0, rows, pressure_column, 0)

    def east_row(e, _):
        v = (wet[e] * wet[e + 1]) * (
            fld[0, e] + DT_FLOW * (CORIOLIS * fld[1, e] - (prs[e + 1] - prs[e]))
        )
        vel[0, e] = v
        cour_e[e] = COURANT * jnp.tanh(v)
        return 0

    lax.fori_loop(0, rows + 1, east_row, 0)

    def north_group(p, _):
        pack = jnp.zeros((lev, LANES), jnp.float32)
        for i in range(sub):
            r = sub * p + i
            w, h, ps, ph = wet[r + 1], weth[r], prs[r + 1], prsh[r]
            v = (w * ahead_of(w, h, lane16)) * (
                fld[1, r + 1]
                + DT_FLOW * (-CORIOLIS * fld[0, r + 1] - (ahead_of(ps, ph, lane16) - ps))
            )
            vel[1, r + 1] = v
            cour_n[r] = COURANT * jnp.tanh(v)
            before = (w * h) * (
                fldh[1, r] + DT_FLOW * (-CORIOLIS * fldh[0, r] - (ps - ph))
            )
            pack = jnp.where(
                lane16 == i, jnp.broadcast_to(before[:, 0:1], (lev, LANES)), pack
            )
        cour_p[p] = COURANT * jnp.tanh(pack)
        return 0

    lax.fori_loop(0, nc, north_group, 0)

    mine = pl.ds(pl.multiple_of(c * lev, lev), lev)
    velocity_copies = []
    for d, peer in enumerate(peers):
        p = peer["comp"]
        for n, (src, dst) in enumerate(
            (
                (cour_e.at[pl.ds(sub * p, sub + 1)], cer.at[:, mine, :]),
                (cour_n.at[pl.ds(sub * p, sub)], cnr.at[:, mine, :]),
                (cour_p.at[p], cpr.at[mine, :]),
            )
        ):
            velocity_copies.append(remote(src, dst, as_s.at[d, n], as_r.at[d, n], peer))
    for copy in velocity_copies:
        copy.start()
    for k in range(4, nchunk):
        send_edges(0, k)
    for i in range(sub + 1):
        cer[i, mine, :] = cour_e[sub * c + i]
    for i in range(sub):
        cnr[i, mine, :] = cour_n[sub * c + i]
    cpr[mine, :] = cour_p[c]

    def store_rows(r, _):
        pltpu.make_async_copy(vel.at[0, r + 1], east_out.at[:, r, 0, :], osem.at[0]).start()
        pltpu.make_async_copy(vel.at[1, r + 1], north_out.at[:, r, 0, :], osem.at[1]).start()
        pltpu.make_async_copy(mixed.at[1, r], salt_out.at[:, r, 0, :], osem.at[2]).start()
        return 0

    lax.fori_loop(0, rows, store_rows, 0)

    for copy in velocity_copies:
        copy.wait_recv()

    def wet_chunk(k, r):
        depth = reach(mb[0, sub * c + r + 1], mb[1, sub * c + r + 1])
        return jnp.where((level8 + k * GROUP).astype(jnp.float32) < depth, 1.0, 0.0)

    def coefficients(k):
        for r in range(sub):
            ce, cw, cn = cer[r + 1, chunk(k), :], cer[r, chunk(k), :], cnr[r, chunk(k), :]
            edge = cpr[chunk(k), :]
            if r:
                edge = pltpu.roll(edge, LANES - r, 1)
            cs = behind_of(cn, edge, lane8)
            w = wet_chunk(k, r)
            out_e, in_e = jnp.maximum(ce, 0.0), jnp.minimum(ce, 0.0)
            out_w, in_w = jnp.maximum(cw, 0.0), jnp.minimum(cw, 0.0)
            out_n, in_n = jnp.maximum(cn, 0.0), jnp.minimum(cn, 0.0)
            out_s, in_s = jnp.maximum(cs, 0.0), jnp.minimum(cs, 0.0)
            wcol[r, chunk(k), :] = w
            coef[0, r, chunk(k), :] = w * (1.0 - (out_e - in_w) - (out_n - in_s))
            coef[1, r, chunk(k), :] = -w * in_e
            coef[2, r, chunk(k), :] = w * out_w
            coef[3, r, chunk(k), :] = -w * in_n
            coef[4, r, chunk(k), :] = w * out_s

    def substep(k, src, dst, stage, each):
        cf = [[coef[i, r, chunk(k), :] for i in range(5)] for r in range(sub)]
        both = [
            merged(hrecv[stage, 1, p, chunk(k), :], hrecv[stage, 0, p, chunk(k), :], lane8)
            for p in range(sub // 2)
        ]
        for t in range(ntr):
            q = [lo[stage, t, chunk(k), :]]
            q += [src[t, r, chunk(k), :] for r in range(sub)]
            q += [hi[stage, t, chunk(k), :]]
            for r in range(sub):
                x = q[r + 1]
                h = slot_of(both[r // 2], 64 * (r % 2) + 2 * t)
                new = (
                    cf[r][0] * x
                    + cf[r][1] * q[r + 2]
                    + cf[r][2] * q[r]
                    + cf[r][3] * ahead_of(x, h, lane8)
                    + cf[r][4] * behind_of(x, h, lane8)
                )
                dst[t, r, chunk(k), :] = new
                each(t, r, new)

    def first_substep(k, _):
        for copy in edge_copies(0, k):
            copy.wait_recv()
        for copy in side_copies(0, k):
            copy.wait_recv()
        coefficients(k)
        packs = [jnp.zeros((GROUP, LANES), jnp.float32) for _ in range(sub // 2)]

        def each(t, r, new):
            packs[r // 2] = packed(packs[r // 2], new, 64 * (r % 2) + 2 * t, lane8)

        substep(k, q0, q1, 0, each)
        for p in range(sub // 2):
            hsend[1, p, chunk(k), :] = packs[p]
        send_edges(1, k)
        send_sides(1, k)
        return 0

    lax.fori_loop(0, nchunk, first_substep, 0)

    layer = 2.0 / levels
    block = 4
    carry[...] = jnp.zeros_like(carry)

    def second_substep(k):
        for copy in edge_copies(1, k):
            copy.wait_recv()
        for copy in side_copies(1, k):
            copy.wait_recv()
        optical = [jnp.zeros((GROUP, LANES), jnp.float32) for _ in range(sub)]

        def each(t, r, new):
            optical[r] = optical[r] + absorb_ref[t] * new

        substep(k, q1, q0, 1, each)
        light, scaled, nutrient = [], [], []
        for r in range(sub):
            step = layer * (CLEAR_WATER + optical[r])
            above = jnp.where(level8 >= 1, pltpu.roll(step, 1, 0), 0.0)
            for d in (1, 2, 4):
                above = above + jnp.where(level8 >= d, pltpu.roll(above, d, 0), 0.0)
            before = carry[r]
            carry[r] = before + jnp.sum(step, axis=0, keepdims=True)
            arriving = sun_ref[r] * jnp.exp(-(before + above))
            warm[r, chunk(k), :] = (
                wcol[r, chunk(k), :] * arriving * (1.0 - jnp.exp(-step)) / layer
            )
            light.append(arriving * jnp.exp(-0.5 * step))
            nutrient.append(q0[0, r, chunk(k), :])
            scaled.append(nutrient[r] * light[r])
        for t in range(ntr):
            for r in range(sub):
                below = (half_ref[t] + nutrient[r]) * (light[r] + light_half_ref[t])
                upt[t, r] = (growth_ref[t] * scaled[r]) * q0[t, r, chunk(k), :] / below
        half_wet = [DT_BIO * wcol[r, chunk(k), :] for r in range(sub)]

        def react(b, _):
            sums = [[jnp.zeros((GROUP, LANES), jnp.float32)] * sub for _ in range(block)]
            for t in range(ntr):
                u = [upt[t, r] for r in range(sub)]
                for i in range(block):
                    s = stoich_ref[block * b + i, t]
                    sums[i] = [sums[i][r] + s * u[r] for r in range(sub)]
            for i in range(block):
                for r in range(sub):
                    res[block * b + i, r, chunk(k), :] = (
                        q0[block * b + i, r, chunk(k), :] + half_wet[r] * sums[i][r]
                    )
            return 0

        lax.fori_loop(0, ntr // block, react, 0)
        for r in range(sub):
            pltpu.make_async_copy(
                res.at[:, r, chunk(k), :], result_out.at[:, chunk(k), r, 0, :], osem.at[3]
            ).start()

    def heat_copy(p):
        part = pl.ds(pl.multiple_of(p * lev, lev), lev)
        return remote(
            warm.at[:, part, :],
            heat.at[pl.ds(sub * c, sub)],
            ws_s.at[p],
            ws_r.at[c],
            {"comp": p, "gx": g, "gy": y},
        )

    def group_of_levels(p, _):
        def one(i, _):
            second_substep(p * (lev // GROUP) + i)
            return 0

        lax.fori_loop(0, lev // GROUP, one, 0)

        @pl.when(p != c)
        def _():
            heat_copy(p).start()

        @pl.when(p == c)
        def _():
            part = pl.ds(pl.multiple_of(p * lev, lev), lev)
            for r in range(sub):
                heat[sub * c + r] = warm[r, part, :]

        return 0

    lax.fori_loop(0, nc, group_of_levels, 0)

    for d in range(1, nc):
        p = lax.rem(c + nc - d, nc)
        remote(
            warm.at[:, pl.ds(0, lev), :],
            heat.at[pl.ds(sub * p, sub)],
            ws_s.at[p],
            ws_r.at[p],
            {"comp": p, "gx": g, "gy": y},
        ).wait_recv()

    def final_row(r, _):
        warmed = mixed[0, r] + WARMING_FACTOR * heat[r]
        fin[0, r] = warmed
        fin[1, r] = wet[r + 1] * (0.2 * warmed - 0.8 * mixed[1, r])
        return 0

    lax.fori_loop(0, rows, final_row, 0)

    def store_final(r, _):
        pltpu.make_async_copy(fin.at[0, r], warmed_out.at[:, r, 0, :], osem.at[4]).start()
        pltpu.make_async_copy(fin.at[1, r], buoy_out.at[:, r, 0, :], osem.at[5]).start()
        return 0

    lax.fori_loop(0, rows, store_final, 0)

    for copy in first + list(column_copies) + total_copies + velocity_copies:
        copy.wait_send()

    def drain(k, _):
        for stage in range(2):
            for copy in edge_copies(stage, k) + side_copies(stage, k):
                copy.wait_send()
        return 0

    lax.fori_loop(0, nchunk, drain, 0)
    for d in range(1, nc):
        heat_copy(lax.rem(c + d, nc)).wait_send()
    for n, ref in enumerate(
        (vel.at[0, pl.ds(1, rows)], vel.at[1, pl.ds(1, rows)], mixed.at[1], res, fin.at[0], fin.at[1])
    ):
        pltpu.make_async_copy(ref, ref, osem.at[n]).wait()


def on_device(mesh_shape, *args):
    (
        zonal,
        merid,
        therm,
        brine,
        mask,
        bottom,
        tracers,
        sun,
        absorb,
        growth,
        half,
        light_half,
        stoich,
    ) = args
    lev, rows, lanes = zonal.shape
    ntr, levels, sub = tracers.shape[0], tracers.shape[1], tracers.shape[4]
    nc, ng, ny = mesh_shape
    nchunk = levels // GROUP
    f32, i32 = jnp.float32, jnp.int32
    column = (lev, rows, 1, lanes)
    vm, dma = pltpu.VMEM, pltpu.SemaphoreType.DMA
    anywhere = pl.BlockSpec(memory_space=pl.ANY)
    in_vmem = pl.BlockSpec(memory_space=pltpu.VMEM)
    in_smem = pl.BlockSpec(memory_space=pltpu.SMEM)
    scratch = [
        vm((4, rows + 2, lev, lanes), f32),
        vm((4, rows, lev, lanes), f32),
        vm((2, rows + 2, 1, lanes), i32),
        vm((2, 2, rows, 1, lanes), i32),
        vm((rows + 2, lev, lanes), f32),
        vm((rows, lev, lanes), f32),
        vm((rows + 2, lev, lanes), f32),
        vm((rows, lev, lanes), f32),
        vm((nc, 2 * rows + 2, 1, lanes), f32),
        vm((rows + 2, lev, lanes), f32),
        vm((rows, lev, lanes), f32),
        vm((2, rows + 1, lev, lanes), f32),
        vm((rows + 1, lev, lanes), f32),
        vm((rows, lev, lanes), f32),
        vm((nc, lev, lanes), f32),
        vm((sub + 1, levels, lanes), f32),
        vm((sub, levels, lanes), f32),
        vm((levels, lanes), f32),
        vm((lev, lanes), f32),
        vm((2, lev, lanes), f32),
        vm((2, rows, lev, lanes), f32),
        vm((rows, lev, lanes), f32),
        vm((2, rows, lev, lanes), f32),
        vm((ntr, sub, levels, lanes), f32),
        vm((ntr, sub, levels, lanes), f32),
        vm((ntr, sub, levels, lanes), f32),
        vm((2, ntr, levels, lanes), f32),
        vm((2, ntr, levels, lanes), f32),
        vm((2, sub // 2, levels, lanes), f32),
        vm((2, 2, sub // 2, levels, lanes), f32),
        vm((5, sub, levels, lanes), f32),
        vm((sub, levels, lanes), f32),
        vm((sub, levels, lanes), f32),
        vm((sub, GROUP, lanes), f32),
        vm((ntr, sub, GROUP, lanes), f32),
        dma((6 + nchunk,)),
        dma((6,)),
        dma((14,)),
        dma((14,)),
        dma((2,)),
        dma((2,)),
        dma((nc - 1,)),
        dma((nc - 1,)),
        dma((nc - 1, 3)),
        dma((nc - 1, 3)),
        dma((2, 2, nchunk)),
        dma((2, 2, nchunk)),
        dma((2, 2, nchunk)),
        dma((2, 2, nchunk)),
        dma((nc,)),
        dma((nc,)),
    ]
    outs = pl.pallas_call(
        functools.partial(ocean_kernel, (ntr, levels, rows, lev, sub, ng, ny)),
        out_shape=[jax.ShapeDtypeStruct(column, f32)] * 5
        + [jax.ShapeDtypeStruct((ntr, levels, sub, 1, lanes), f32)],
        in_specs=[anywhere] * 7 + [in_vmem] + [in_smem] * 5,
        out_specs=[anywhere] * 6,
        scratch_shapes=scratch,
        compiler_params=pltpu.CompilerParams(
            collective_id=0, has_side_effects=True, vmem_limit_bytes=48 << 20
        ),
        name="ocean",
    )(
        *(x.reshape(column) for x in (zonal, merid, therm, brine)),
        mask.reshape(rows, 1, lanes),
        bottom.reshape(rows, 1, lanes),
        tracers.reshape(ntr, levels, sub, 1, lanes),
        sun.reshape(sub, 1, lanes),
        absorb,
        growth,
        half,
        light_half,
        stoich,
    )
    return tuple(x.reshape(zonal.shape) for x in outs[:5]) + (outs[5].reshape(tracers.shape),)


def solution(mesh):
    field = P("comp", "gx", "gy")
    tile = P("gx", "gy")
    tracer = P(None, None, "gx", "comp", None, "gy")
    shape = tuple(mesh.shape[a] for a in ("comp", "gx", "gy"))
    return jax.shard_map(
        functools.partial(on_device, shape),
        mesh=mesh,
        in_specs=(field,) * 4 + (tile,) * 2 + (tracer, P("gx", "comp", None, "gy")) + (P(),) * 5,
        out_specs=(field,) * 5 + (tracer,),
        check_vma=False,
    )
```

time: 254 us -> 103 us (0.41)
  the two profiles are of different devices: /device:TPU:15 before, /device:TPU:24 now
where the time goes in v1:
time: 103 us; the launch traced here: 101 us
  Pallas kernels  86.4 us (84%)
  local copies, waits for them, and re-layouts  13.9 us (13%)
    pallas_call x1, Pallas kernels, on_device(): pl.pallas_call(functools.partial(ocean_kernel, (ntr, levels, rows, lev, s...  86.4 us
    unnamed x30, local copies, waits for them, and re-layouts  13.9 us

profile of v1, /device:TPU:24, one launch (start us, length us, event | category | flops | bytes accessed | tf_op | source)
XLA Modules:
  0.0 101.0 jit_solution(17764173113092926078)
XLA Ops:
  0.6 0.0 copy-start
  0.6 0.9 copy-done
  1.5 0.0 copy-start.1
  1.5 0.9 copy-done.1
  2.4 0.0 copy-start.2
  2.4 0.9 copy-done.2
  3.4 0.0 copy-start.3
  3.4 0.9 copy-done.3
  4.3 0.0 copy-start.4
  4.3 0.7 copy-done.4
  5.0 0.0 copy-start.5
  5.0 0.7 copy-done.5
  5.7 0.0 copy-start.6
  5.7 0.7 copy-done.6
  6.4 0.0 copy-start.7
  6.4 0.7 copy-done.7
  7.0 0.0 copy-start.8
  7.0 0.7 copy-done.8
  7.7 0.0 copy-start.9
  7.7 0.7 copy-done.9
  8.4 0.0 copy-start.10
  8.4 0.7 copy-done.10
  9.0 0.0 copy-start.11
  9.0 0.7 copy-done.11
  9.7 86.4 %ocean.1 = (f32[16,16,1,128]{3,2,1,0:T(1,128)S(1)}, f32[16,16,1,128]{3,2,1,0:T(1,128)S(1)}, f32[16,16,1,128]{3,2,1,0:T(1,128)S(1)}, f32[16,16,1,128]{3,2,1,0:T(1...) custom-call(f32[16,16,1,128]{3,2,1,0:T(1,128)S(1)} %bitcast.17, ...), custom_call_target="tpu_custom_call" | custom-call | tf_op jit(solution)/shard_map/ocean/pallas_call | solution.py:702
  96.1 0.7 copy.26
  96.7 0.7 copy.27
  97.4 0.7 copy.28
  98.0 0.7 copy.29
  98.7 0.7 copy.30
  99.3 1.7 %copy.31 = f32[24,64,1,1,4,128]{5,4,3,2,1,0:T(4,128)} copy(f32[24,64,1,1,4,128]{5,4,3,2,1,0:T(4,128)S(1)} %bitcast.16) | data formatting | bytes 6291456
Async XLA Ops:
  0.6 0.9 copy-start
  1.5 0.9 copy-start.1
  2.4 0.9 copy-start.2
  3.4 0.9 copy-start.3
  4.3 0.7 copy-start.4
  5.0 0.7 copy-start.5
  5.7 0.7 copy-start.6
  6.4 0.7 copy-start.7
  7.0 0.7 copy-start.8
  7.7 0.7 copy-start.9
  8.4 0.7 copy-start.10
  9.0 0.7 copy-start.11

commit v2 on v1

--- a/solution.py
+++ b/solution.py
@@ -10,6 +10,7 @@
 MESH = pl.DeviceIdType.MESH
 LANES = 128
 GROUP = 8
+DEPTH = 2
 
 DT_FLOW = 0.1
 CORIOLIS = 0.3
@@ -29,12 +30,12 @@
     mask_ref,
     bottom_ref,
     tracer_ref,
-    sun_ref,
-    absorb_ref,
-    growth_ref,
-    half_ref,
-    light_half_ref,
-    stoich_ref,
+    sun_in,
+    absorb_in,
+    growth_in,
+    half_in,
+    light_half_in,
+    stoich_in,
     east_out,
     north_out,
     warmed_out,
@@ -76,6 +77,12 @@
     warm,
     carry,
     upt,
+    sun_ref,
+    absorb_ref,
+    growth_ref,
+    half_ref,
+    light_half_ref,
+    stoich_ref,
     lsem,
     osem,
     p1s,
@@ -126,6 +133,11 @@
     def chunk(k):
         return pl.ds(pl.multiple_of(k * GROUP, GROUP), GROUP)
 
+    barrier = pltpu.get_barrier_semaphore()
+    partners = [up, down, gxp, gxm, gyp, gym] + peers
+    for device in partners:
+        pl.semaphore_signal(barrier, inc=1, device_id=device, device_id_type=MESH)
+
     fields = (zonal_ref, merid_ref, therm_ref, brine_ref)
 
     def load_rows(r, _):
@@ -145,11 +157,22 @@
         return 0
 
     lax.fori_loop(0, nchunk, load_tracers, 0)
-
-    barrier = pltpu.get_barrier_semaphore()
-    partners = [up, down, gxp, gxm, gyp, gym] + peers
-    for device in partners:
-        pl.semaphore_signal(barrier, inc=1, device_id=device, device_id_type=MESH)
+    settings = [
+        pltpu.make_async_copy(src, dst, lsem.at[6 + nchunk + n])
+        for n, (src, dst) in enumerate(
+            (
+                (sun_in, sun_ref),
+                (absorb_in, absorb_ref),
+                (growth_in, growth_ref),
+                (half_in, half_ref),
+                (light_half_in, light_half_ref),
+                (stoich_in, stoich_ref),
+            )
+        )
+    ]
+    for copy in settings:
+        copy.start()
+
     pl.semaphore_wait(barrier, len(partners))
 
     first = []
@@ -211,9 +234,6 @@
         for copy in side_copies(stage, k):
             copy.start()
 
-    send_edges(0, 0)
-    send_edges(0, 1)
-
     lane16 = lax.broadcasted_iota(jnp.int32, (lev, LANES), 1)
     level16 = lax.broadcasted_iota(jnp.int32, (lev, LANES), 0)
     depth16 = (level16 + c * lev).astype(jnp.float32)
@@ -271,17 +291,19 @@
 
     lax.fori_loop(0, rows, own_row, 0)
 
+    def pack_chunk(stage, src, k):
+        for pair in range(sub // 2):
+            a = jnp.zeros((GROUP, LANES), jnp.float32)
+            for half in range(2):
+                for t in range(ntr):
+                    a = packed(a, src[t, 2 * pair + half, chunk(k), :], 64 * half + 2 * t, lane8)
+            hsend[stage, pair, chunk(k), :] = a
+
     def pack_sides(k, _):
         pltpu.make_async_copy(
             q0.at[:, :, chunk(k), :], q0.at[:, :, chunk(k), :], lsem.at[6 + k]
         ).wait()
-        for pair in range(sub // 2):
-            a = jnp.zeros((GROUP, LANES), jnp.float32)
-            for half in range(2):
-                for t in range(ntr):
-                    a = packed(a, q0[t, 2 * pair + half, chunk(k), :], 64 * half + 2 * t, lane8)
-            hsend[0, pair, chunk(k), :] = a
-        send_sides(0, k)
+        pack_chunk(0, q0, k)
         return 0
 
     lax.fori_loop(0, nchunk, pack_sides, 0)
@@ -316,23 +338,6 @@
     ]
     for copy in total_copies:
         copy.start()
-    send_edges(0, 2)
-    send_edges(0, 3)
-
-    def mixing_row(r, _):
-        w, h = wet[r + 1], weth[r]
-        open_e, open_w = w * wet[r + 2], wet[r] * w
-        open_n, open_s = w * ahead_of(w, h, lane16), w * behind_of(w, h, lane16)
-        for i in range(2):
-            x, xh = fld[2 + i, r + 1], fldh[2 + i, r]
-            flux_e = open_e * (fld[2 + i, r + 2] - x)
-            flux_w = open_w * (x - fld[2 + i, r])
-            flux_n = open_n * (ahead_of(x, xh, lane16) - x)
-            flux_s = open_s * (x - behind_of(x, xh, lane16))
-            mixed[i, r] = x + MIXING * ((flux_e - flux_w) + (flux_n - flux_s))
-        return 0
-
-    lax.fori_loop(0, rows, mixing_row, 0)
 
     for d, peer in enumerate(peers):
         total_copies[d].wait_recv()
@@ -405,13 +410,29 @@
             velocity_copies.append(remote(src, dst, as_s.at[d, n], as_r.at[d, n], peer))
     for copy in velocity_copies:
         copy.start()
-    for k in range(4, nchunk):
+    for k in range(DEPTH):
+        send_sides(0, k)
         send_edges(0, k)
     for i in range(sub + 1):
         cer[i, mine, :] = cour_e[sub * c + i]
     for i in range(sub):
         cnr[i, mine, :] = cour_n[sub * c + i]
     cpr[mine, :] = cour_p[c]
+
+    def mixing_row(r, _):
+        w, h = wet[r + 1], weth[r]
+        open_e, open_w = w * wet[r + 2], wet[r] * w
+        open_n, open_s = w * ahead_of(w, h, lane16), w * behind_of(w, h, lane16)
+        for i in range(2):
+            x, xh = fld[2 + i, r + 1], fldh[2 + i, r]
+            flux_e = open_e * (fld[2 + i, r + 2] - x)
+            flux_w = open_w * (x - fld[2 + i, r])
+            flux_n = open_n * (ahead_of(x, xh, lane16) - x)
+            flux_s = open_s * (x - behind_of(x, xh, lane16))
+            mixed[i, r] = x + MIXING * ((flux_e - flux_w) + (flux_n - flux_s))
+        return 0
+
+    lax.fori_loop(0, rows, mixing_row, 0)
 
     def store_rows(r, _):
         pltpu.make_async_copy(vel.at[0, r + 1], east_out.at[:, r, 0, :], osem.at[0]).start()
@@ -470,26 +491,25 @@
                 dst[t, r, chunk(k), :] = new
                 each(t, r, new)
 
-    def first_substep(k, _):
+    def first_substep(k):
         for copy in edge_copies(0, k):
             copy.wait_recv()
         for copy in side_copies(0, k):
             copy.wait_recv()
         coefficients(k)
-        packs = [jnp.zeros((GROUP, LANES), jnp.float32) for _ in range(sub // 2)]
-
-        def each(t, r, new):
-            packs[r // 2] = packed(packs[r // 2], new, 64 * (r % 2) + 2 * t, lane8)
-
-        substep(k, q0, q1, 0, each)
-        for p in range(sub // 2):
-            hsend[1, p, chunk(k), :] = packs[p]
+        substep(k, q0, q1, 0, lambda t, r, new: None)
         send_edges(1, k)
+        pack_chunk(1, q1, k)
         send_sides(1, k)
-        return 0
-
-    lax.fori_loop(0, nchunk, first_substep, 0)
-
+
+        @pl.when(k + DEPTH < nchunk)
+        def _():
+            send_sides(0, k + DEPTH)
+            send_edges(0, k + DEPTH)
+
+
+    for copy in settings:
+        copy.wait()
     layer = 2.0 / levels
     block = 4
     carry[...] = jnp.zeros_like(carry)
@@ -556,13 +576,7 @@
             {"comp": p, "gx": g, "gy": y},
         )
 
-    def group_of_levels(p, _):
-        def one(i, _):
-            second_substep(p * (lev // GROUP) + i)
-            return 0
-
-        lax.fori_loop(0, lev // GROUP, one, 0)
-
+    def send_heat(p):
         @pl.when(p != c)
         def _():
             heat_copy(p).start()
@@ -573,9 +587,24 @@
             for r in range(sub):
                 heat[sub * c + r] = warm[r, part, :]
 
-        return 0
-
-    lax.fori_loop(0, nc, group_of_levels, 0)
+    each_peer = lev // GROUP
+
+    def advance(k, _):
+        @pl.when(k < nchunk)
+        def _():
+            first_substep(k)
+
+        @pl.when(k > 0)
+        def _():
+            second_substep(k - 1)
+
+        @pl.when((k > 0) & (lax.rem(k, each_peer) == 0))
+        def _():
+            send_heat(k // each_peer - 1)
+
+        return 0
+
+    lax.fori_loop(0, nchunk + 1, advance, 0)
 
     for d in range(1, nc):
         p = lax.rem(c + nc - d, nc)
@@ -618,6 +647,35 @@
         (vel.at[0, pl.ds(1, rows)], vel.at[1, pl.ds(1, rows)], mixed.at[1], res, fin.at[0], fin.at[1])
     ):
         pltpu.make_async_copy(ref, ref, osem.at[n]).wait()
+
+
+def place_kernel(count, *refs):
+    sources, targets = refs[:count], refs[count : 2 * count]
+    held, sems = refs[2 * count : 3 * count], refs[3 * count]
+    parts = 8
+    copies = []
+    for n in range(count):
+        size = sources[n].shape[0] // parts
+        for p in range(parts):
+            part = pl.ds(p * size, size)
+            copies.append(
+                (
+                    pltpu.make_async_copy(
+                        sources[n].at[part], held[n].at[part], sems.at[0, n, p]
+                    ),
+                    pltpu.make_async_copy(
+                        held[n].at[part], targets[n].at[part], sems.at[1, n, p]
+                    ),
+                )
+            )
+    copies = copies[(count - 1) * parts :] + copies[: (count - 1) * parts]
+    for fetch, _ in copies:
+        fetch.start()
+    for fetch, put in copies:
+        fetch.wait()
+        put.start()
+    for _, put in copies:
+        put.wait()
 
 
 def on_device(mesh_shape, *args):
@@ -644,8 +702,6 @@
     column = (lev, rows, 1, lanes)
     vm, dma = pltpu.VMEM, pltpu.SemaphoreType.DMA
     anywhere = pl.BlockSpec(memory_space=pl.ANY)
-    in_vmem = pl.BlockSpec(memory_space=pltpu.VMEM)
-    in_smem = pl.BlockSpec(memory_space=pltpu.SMEM)
     scratch = [
         vm((4, rows + 2, lev, lanes), f32),
         vm((4, rows, lev, lanes), f32),
@@ -682,7 +738,13 @@
         vm((sub, levels, lanes), f32),
         vm((sub, GROUP, lanes), f32),
         vm((ntr, sub, GROUP, lanes), f32),
-        dma((6 + nchunk,)),
+        vm((sub, 1, lanes), f32),
+        pltpu.SMEM((ntr,), f32),
+        pltpu.SMEM((ntr,), f32),
+        pltpu.SMEM((ntr,), f32),
+        pltpu.SMEM((ntr,), f32),
+        pltpu.SMEM((ntr, ntr), f32),
+        dma((12 + nchunk,)),
         dma((6,)),
         dma((14,)),
         dma((14,)),
@@ -703,11 +765,11 @@
         functools.partial(ocean_kernel, (ntr, levels, rows, lev, sub, ng, ny)),
         out_shape=[jax.ShapeDtypeStruct(column, f32)] * 5
         + [jax.ShapeDtypeStruct((ntr, levels, sub, 1, lanes), f32)],
-        in_specs=[anywhere] * 7 + [in_vmem] + [in_smem] * 5,
+        in_specs=[anywhere] * 13,
         out_specs=[anywhere] * 6,
         scratch_shapes=scratch,
         compiler_params=pltpu.CompilerParams(
-            collective_id=0, has_side_effects=True, vmem_limit_bytes=48 << 20
+            collective_id=0, has_side_effects=True, vmem_limit_bytes=67043328
         ),
         name="ocean",
     )(
@@ -722,7 +784,19 @@
         light_half,
         stoich,
     )
-    return tuple(x.reshape(zonal.shape) for x in outs[:5]) + (outs[5].reshape(tracers.shape),)
+    outs = [x.reshape(zonal.shape) for x in outs[:5]] + [outs[5].reshape(tracers.shape)]
+    count = len(outs)
+    return tuple(
+        pl.pallas_call(
+            functools.partial(place_kernel, count),
+            out_shape=[jax.ShapeDtypeStruct(x.shape, f32) for x in outs],
+            in_specs=[anywhere] * count,
+            out_specs=[anywhere] * count,
+            scratch_shapes=[vm(x.shape, f32) for x in outs] + [dma((2, count, 8))],
+            compiler_params=pltpu.CompilerParams(vmem_limit_bytes=67043328),
+            name="place",
+        )(*outs)
+    )
 
 
 def solution(mesh):

time: 103 us -> 81.9 us (0.80)
  the two profiles are of different devices: /device:TPU:24 before, /device:TPU:62 now
where the time goes in v2:
time: 81.9 us; the launch traced here: 81.8 us
  Pallas kernels  81.2 us (99%)
    pallas_call x1, Pallas kernels, on_device(): pl.pallas_call(functools.partial(ocean_kernel, (ntr, levels, rows, lev, s...  77.5 us
    pallas_call x1, Pallas kernels, on_device(): pl.pallas_call(functools.partial(place_kernel, count), out_shape=[jax.Sha...  3.7 us

profile of v2, /device:TPU:62, one launch (start us, length us, event | category | flops | bytes accessed | tf_op | source)
XLA Modules:
  0.0 81.8 jit_solution(17223118237651591727)
XLA Ops:
  0.6 77.5 %ocean.1 = (f32[16,16,1,128]{3,2,1,0:T(1,128)}, f32[16,16,1,128]{3,2,1,0:T(1,128)}, f32[16,16,1,128]{3,2,1,0:T(1,128)}, f32[16,16,1,128]{3,2,1,0:T(1,128)}, f32[...) custom-call(f32[16,16,1,128]{3,2,1,0:T(1,128)} %bitcast.16, f32[16,16,1,128]{3,2,1,0:T(1,128)} %bitcast.17, ...), custom_call_target="tpu_custom_call" | custom-call | tf_op jit(solution)/shard_map/ocean/pallas_call | solution.py:764
  78.1 3.7 %place.1 = (f32[16,16,128]{2,1,0:T(8,128)}, f32[16,16,128]{2,1,0:T(8,128)}, f32[16,16,128]{2,1,0:T(8,128)}, f32[16,16,128]{2,1,0:T(8,128)}, f32[16,16,128]{2,1,0:T(8,128)}, /*index=5*/f32[24,64,1,1,4,128]{5,4,3,2,1,0:T(4,128)}) custom-call(f32[16,16,128]{2,1,0:T(8,128)} %bitcast.20, f32[16,16,128]{2,1,0:T(8,128)} %bitcast.21, f32[16,16,128]{2,1,0:T(8,128)} %bitcast.22, ...), custom_call_target="tpu_custom_call" | custom-call | tf_op jit(solution)/shard_map/place/pallas_call | solution.py:790

commit v3 on v2

--- a/solution.py
+++ b/solution.py
@@ -10,7 +10,7 @@
 MESH = pl.DeviceIdType.MESH
 LANES = 128
 GROUP = 8
-DEPTH = 2
+DEPTH = 3
 
 DT_FLOW = 0.1
 CORIOLIS = 0.3
@@ -51,6 +51,7 @@
     den,
     denh,
     tot,
+    toty,
     prs,
     prsh,
     vel,
@@ -135,6 +136,9 @@
 
     barrier = pltpu.get_barrier_semaphore()
     partners = [up, down, gxp, gxm, gyp, gym] + peers
+    for peer in peers:
+        p = peer["comp"]
+        partners += [{**near, "comp": p} for near in (gxp, gxm, gyp, gym)]
     for device in partners:
         pl.semaphore_signal(barrier, inc=1, device_id=device, device_id_type=MESH)
 
@@ -234,6 +238,9 @@
         for copy in side_copies(stage, k):
             copy.start()
 
+    for k in range(1):
+        send_edges(0, k)
+
     lane16 = lax.broadcasted_iota(jnp.int32, (lev, LANES), 1)
     level16 = lax.broadcasted_iota(jnp.int32, (lev, LANES), 0)
     depth16 = (level16 + c * lev).astype(jnp.float32)
@@ -291,6 +298,27 @@
 
     lax.fori_loop(0, rows, own_row, 0)
 
+    def total_copies(source, p):
+        whole = tot.at[source, pl.ds(1, rows)]
+        sends = (
+            (whole, whole, {"gx": g, "gy": y}),
+            (tot.at[source, pl.ds(rows, 1)], tot.at[source, pl.ds(0, 1)], gxp),
+            (tot.at[source, pl.ds(1, 1)], tot.at[source, pl.ds(rows + 1, 1)], gxm),
+            (whole, toty.at[0, source], gyp),
+            (whole, toty.at[1, source], gym),
+        )
+        return [
+            remote(src, dst, ts_s.at[n, p], ts_r.at[n, source], {**device, "comp": p})
+            for n, (src, dst, device) in enumerate(sends)
+        ]
+
+    for p in range(1, nc):
+
+        @pl.when(p > c)
+        def _(p=p):
+            for copy in total_copies(c, p):
+                copy.start()
+
     def pack_chunk(stage, src, k):
         for pair in range(sub // 2):
             a = jnp.zeros((GROUP, LANES), jnp.float32)
@@ -329,36 +357,39 @@
         d = w * (-0.2 * fldh[2, r] + 0.8 * fldh[3, r])
         weth[r] = w
         denh[r] = d
-        tot[c, rows + 2 + r] = jnp.sum(d, axis=0, keepdims=True)
         return 0
 
     lax.fori_loop(0, rows, halo_columns, 0)
-    total_copies = [
-        remote(tot.at[c], tot.at[c], ts_s.at[d], ts_r.at[d], peer) for d, peer in enumerate(peers)
-    ]
-    for copy in total_copies:
-        copy.start()
-
-    for d, peer in enumerate(peers):
-        total_copies[d].wait_recv()
-
-    def pressure_of(d, e):
+
+    for p in range(nc - 1):
+
+        @pl.when(p < c)
+        def _(p=p):
+            for copy in total_copies(p, p):
+                copy.wait_recv()
+
+    def running(d):
         incl = d
         step = 1
         while step < lev:
             incl = incl + jnp.where(level16 >= step, pltpu.roll(incl, step, 0), 0.0)
             step *= 2
+        return incl - 0.5 * d
+
+    def levels_above(totals):
         offset = jnp.zeros((1, LANES), jnp.float32)
         for p in range(nc - 1):
-            offset = offset + jnp.where(p < c, tot[p, e], 0.0)
-        return offset + incl - 0.5 * d
+            offset = offset + jnp.where(p < c, totals(p), 0.0)
+        return jnp.broadcast_to(offset, (lev, LANES))
 
     def pressure_row(e, _):
-        prs[e] = pressure_of(den[e], e)
+        prs[e] = levels_above(lambda p: tot[p, e]) + running(den[e])
         return 0
 
     def pressure_column(r, _):
-        prsh[r] = pressure_of(denh[r], rows + 2 + r)
+        behind = pltpu.roll(levels_above(lambda p: toty[0, p, r]), 1, 1)
+        ahead = pltpu.roll(levels_above(lambda p: toty[1, p, r]), LANES - 1, 1)
+        prsh[r] = jnp.where(lane16 == 0, behind, ahead) + running(denh[r])
         return 0
 
     lax.fori_loop(0, rows + 2, pressure_row, 0)
@@ -410,9 +441,8 @@
             velocity_copies.append(remote(src, dst, as_s.at[d, n], as_r.at[d, n], peer))
     for copy in velocity_copies:
         copy.start()
-    for k in range(DEPTH):
+    for k in range(1):
         send_sides(0, k)
-        send_edges(0, k)
     for i in range(sub + 1):
         cer[i, mine, :] = cour_e[sub * c + i]
     for i in range(sub):
@@ -444,6 +474,9 @@
 
     for copy in velocity_copies:
         copy.wait_recv()
+    for k in range(1, DEPTH):
+        send_sides(0, k)
+        send_edges(0, k)
 
     def wet_chunk(k, r):
         depth = reach(mb[0, sub * c + r + 1], mb[1, sub * c + r + 1])
@@ -631,8 +664,14 @@
 
     lax.fori_loop(0, rows, store_final, 0)
 
-    for copy in first + list(column_copies) + total_copies + velocity_copies:
+    for copy in first + list(column_copies) + velocity_copies:
         copy.wait_send()
+    for p in range(1, nc):
+
+        @pl.when(p > c)
+        def _(p=p):
+            for copy in total_copies(c, p):
+                copy.wait_send()
 
     def drain(k, _):
         for stage in range(2):
@@ -711,7 +750,8 @@
         vm((rows, lev, lanes), f32),
         vm((rows + 2, lev, lanes), f32),
         vm((rows, lev, lanes), f32),
-        vm((nc, 2 * rows + 2, 1, lanes), f32),
+        vm((nc, rows + 2, 1, lanes), f32),
+        vm((2, nc, rows, 1, lanes), f32),
         vm((rows + 2, lev, lanes), f32),
         vm((rows, lev, lanes), f32),
         vm((2, rows + 1, lev, lanes), f32),
@@ -750,8 +790,8 @@
         dma((14,)),
         dma((2,)),
         dma((2,)),
-        dma((nc - 1,)),
-        dma((nc - 1,)),
+        dma((5, nc)),
+        dma((5, nc)),
         dma((nc - 1, 3)),
         dma((nc - 1, 3)),
         dma((2, 2, nchunk)),

time: 81.9 us -> 76.2 us (0.930)
  the two profiles are of different devices: /device:TPU:62 before, /device:TPU:24 now
where the time goes in v3:
time: 76.2 us; the launch traced here: 76.1 us
  Pallas kernels  75.5 us (99%)
    pallas_call x1, Pallas kernels, on_device(): pl.pallas_call(functools.partial(ocean_kernel, (ntr, levels, rows, lev, s...  71.8 us
    pallas_call x1, Pallas kernels, on_device(): pl.pallas_call(functools.partial(place_kernel, count), out_shape=[jax.Sha...  3.7 us

profile of v3, /device:TPU:24, one launch (start us, length us, event | category | flops | bytes accessed | tf_op | source)
XLA Modules:
  0.0 76.1 jit_solution(2613552858166900039)
XLA Ops:
  0.6 71.8 %ocean.1 = (f32[16,16,1,128]{3,2,1,0:T(1,128)}, f32[16,16,1,128]{3,2,1,0:T(1,128)}, f32[16,16,1,128]{3,2,1,0:T(1,128)}, f32[16,16,1,128]{3,2,1,0:T(1,128)}, f32[...) custom-call(f32[16,16,1,128]{3,2,1,0:T(1,128)} %bitcast.16, f32[16,16,1,128]{3,2,1,0:T(1,128)} %bitcast.17, ...), custom_call_target="tpu_custom_call" | custom-call | tf_op jit(solution)/shard_map/ocean/pallas_call | solution.py:804
  72.4 3.7 %place.1 = (f32[16,16,128]{2,1,0:T(8,128)}, f32[16,16,128]{2,1,0:T(8,128)}, f32[16,16,128]{2,1,0:T(8,128)}, f32[16,16,128]{2,1,0:T(8,128)}, f32[16,16,128]{2,1,0:T(8,128)}, /*index=5*/f32[24,64,1,1,4,128]{5,4,3,2,1,0:T(4,128)}) custom-call(f32[16,16,128]{2,1,0:T(8,128)} %bitcast.20, f32[16,16,128]{2,1,0:T(8,128)} %bitcast.21, f32[16,16,128]{2,1,0:T(8,128)} %bitcast.22, ...), custom_call_target="tpu_custom_call" | custom-call | tf_op jit(solution)/shard_map/place/pallas_call | solution.py:830

commit v4 on v3

--- a/solution.py
+++ b/solution.py
@@ -361,6 +361,9 @@
 
     lax.fori_loop(0, rows, halo_columns, 0)
 
+    for k in range(1, 2):
+        send_edges(0, k)
+
     for p in range(nc - 1):
 
         @pl.when(p < c)
@@ -441,7 +444,7 @@
             velocity_copies.append(remote(src, dst, as_s.at[d, n], as_r.at[d, n], peer))
     for copy in velocity_copies:
         copy.start()
-    for k in range(1):
+    for k in range(2):
         send_sides(0, k)
     for i in range(sub + 1):
         cer[i, mine, :] = cour_e[sub * c + i]
@@ -474,7 +477,7 @@
 
     for copy in velocity_copies:
         copy.wait_recv()
-    for k in range(1, DEPTH):
+    for k in range(2, DEPTH):
         send_sides(0, k)
         send_edges(0, k)
 

time: 76.2 us -> 74.2 us (0.974)
  Pallas kernels: 75.5 us -> 73.5 us
    pallas_call x1, Pallas kernels: 71.8 us -> 69.8 us  [on_device(): pl.pallas_call(functools.partial(ocean_kernel, (ntr, levels, rows, lev, s...]
where the time goes in v4:
time: 74.2 us; the launch traced here: 74.1 us
  Pallas kernels  73.5 us (99%)
    pallas_call x1, Pallas kernels, on_device(): pl.pallas_call(functools.partial(ocean_kernel, (ntr, levels, rows, lev, s...  69.8 us
    pallas_call x1, Pallas kernels, on_device(): pl.pallas_call(functools.partial(place_kernel, count), out_shape=[jax.Sha...  3.7 us

profile of v4, /device:TPU:24, one launch (start us, length us, event | category | flops | bytes accessed | tf_op | source)
XLA Modules:
  0.0 74.1 jit_solution(12617562361262774249)
XLA Ops:
  0.6 69.8 %ocean.1 = (f32[16,16,1,128]{3,2,1,0:T(1,128)}, f32[16,16,1,128]{3,2,1,0:T(1,128)}, f32[16,16,1,128]{3,2,1,0:T(1,128)}, f32[16,16,1,128]{3,2,1,0:T(1,128)}, f32[...) custom-call(f32[16,16,1,128]{3,2,1,0:T(1,128)} %bitcast.16, f32[16,16,1,128]{3,2,1,0:T(1,128)} %bitcast.17, ...), custom_call_target="tpu_custom_call" | custom-call | tf_op jit(solution)/shard_map/ocean/pallas_call | solution.py:807
  70.4 3.7 %place.1 = (f32[16,16,128]{2,1,0:T(8,128)}, f32[16,16,128]{2,1,0:T(8,128)}, f32[16,16,128]{2,1,0:T(8,128)}, f32[16,16,128]{2,1,0:T(8,128)}, f32[16,16,128]{2,1,0:T(8,128)}, /*index=5*/f32[24,64,1,1,4,128]{5,4,3,2,1,0:T(4,128)}) custom-call(f32[16,16,128]{2,1,0:T(8,128)} %bitcast.20, f32[16,16,128]{2,1,0:T(8,128)} %bitcast.21, f32[16,16,128]{2,1,0:T(8,128)} %bitcast.22, ...), custom_call_target="tpu_custom_call" | custom-call | tf_op jit(solution)/shard_map/place/pallas_call | solution.py:833

commit v5 on v4

--- a/solution.py
+++ b/solution.py
@@ -10,7 +10,7 @@
 MESH = pl.DeviceIdType.MESH
 LANES = 128
 GROUP = 8
-DEPTH = 3
+DEPTH = 2
 
 DT_FLOW = 0.1
 CORIOLIS = 0.3
@@ -477,9 +477,6 @@
 
     for copy in velocity_copies:
         copy.wait_recv()
-    for k in range(2, DEPTH):
-        send_sides(0, k)
-        send_edges(0, k)
 
     def wet_chunk(k, r):
         depth = reach(mb[0, sub * c + r + 1], mb[1, sub * c + r + 1])
@@ -694,9 +691,9 @@
 def place_kernel(count, *refs):
     sources, targets = refs[:count], refs[count : 2 * count]
     held, sems = refs[2 * count : 3 * count], refs[3 * count]
-    parts = 8
     copies = []
     for n in range(count):
+        parts = 8 if n == count - 1 else 1
         size = sources[n].shape[0] // parts
         for p in range(parts):
             part = pl.ds(p * size, size)
@@ -710,7 +707,7 @@
                     ),
                 )
             )
-    copies = copies[(count - 1) * parts :] + copies[: (count - 1) * parts]
+    copies = copies[count - 1 :] + copies[: count - 1]
     for fetch, _ in copies:
         fetch.start()
     for fetch, put in copies:

time: 74.2 us -> 73.6 us (level)
  no operation moved by 1% of the time
where the time goes in v5:
time: 73.6 us; the launch traced here: 73.5 us
  Pallas kernels  72.9 us (99%)
    pallas_call x1, Pallas kernels, on_device(): pl.pallas_call(functools.partial(ocean_kernel, (ntr, levels, rows, lev, s...  69 us
    pallas_call x1, Pallas kernels, on_device(): pl.pallas_call(functools.partial(place_kernel, count), out_shape=[jax.Sha...  3.83 us

profile of v5, /device:TPU:24, one launch (start us, length us, event | category | flops | bytes accessed | tf_op | source)
XLA Modules:
  0.0 73.5 jit_solution(138670163168585590)
XLA Ops:
  0.6 69.0 %ocean.1 = (f32[16,16,1,128]{3,2,1,0:T(1,128)}, f32[16,16,1,128]{3,2,1,0:T(1,128)}, f32[16,16,1,128]{3,2,1,0:T(1,128)}, f32[16,16,1,128]{3,2,1,0:T(1,128)}, f32[...) custom-call(f32[16,16,1,128]{3,2,1,0:T(1,128)} %bitcast.16, f32[16,16,1,128]{3,2,1,0:T(1,128)} %bitcast.17, ...), custom_call_target="tpu_custom_call" | custom-call | tf_op jit(solution)/shard_map/ocean/pallas_call | solution.py:804
  69.7 3.8 %place.1 = (f32[16,16,128]{2,1,0:T(8,128)}, f32[16,16,128]{2,1,0:T(8,128)}, f32[16,16,128]{2,1,0:T(8,128)}, f32[16,16,128]{2,1,0:T(8,128)}, f32[16,16,128]{2,1,0:T(8,128)}, /*index=5*/f32[24,64,1,1,4,128]{5,4,3,2,1,0:T(4,128)}) custom-call(f32[16,16,128]{2,1,0:T(8,128)} %bitcast.20, f32[16,16,128]{2,1,0:T(8,128)} %bitcast.21, f32[16,16,128]{2,1,0:T(8,128)} %bitcast.22, ...), custom_call_target="tpu_custom_call" | custom-call | tf_op jit(solution)/shard_map/place/pallas_call | solution.py:830
